TPU v7x, 32 devices: a whole 2x2x4 slice. The times are simulated.
32 devices in a mesh: row: 4 (over z), col: 8 (over y, x, core).
Axes of the slice: x: 2, y: 2, z: 4, core: 2. Of those that a mesh axis runs over, the one named last changes fastest.
Arguments:
- scans: float32 [4096, 4, 8, 128], P(('row', 'col')), may hold values from -6 to 6
- dest: int32 [4096, 1], P(('row', 'col')), may hold values from 0 to 31; in each aligned block of 128 rows (0 to 127, 128 to 255, ...) at most 8 rows name the same one
- offsets: int32 [4096], P(('row', 'col')), may hold values from 0 to 252
- profile_index: int32 [4096], P(('row', 'col')), may hold values from 0 to 15
- profiles: float32 [16, 4, 128], replicated, may hold values from 0.1 to 1.5
- embed_weight: bfloat16 [512, 1024], replicated, may hold values from -0.25 to 0.25
- attn_gain: float32 [2, 1024], replicated, may hold values from 0.1 to 1.9
- qkv_weight: bfloat16 [2, 1024, 3072], replicated, may hold values from -3 to 3
- out_weight: bfloat16 [2, 1024, 1024], replicated, may hold values from -0.1875 to 0.1875
Outputs:
- tokens: bfloat16 [128, 128, 1024], P('row', 'col')
Inputs may be any that keep to these rules, and one draw needn't show every extreme that they name: dest[b, 0] is the tile of block b, numbered 8 * tile row + tile column; of the 128 blocks of one device at most 8 go to any one tile.
All inputs are finite; a program needn't handle non-finite values.
Results may differ from a plain program's by a relative error of at most 0.012.
Values may be sent and summed in bfloat16 or wider, within the bound.
A program may use at most 128 MiB of HBM per device.

v0:
```python
import math

import jax
import jax.numpy as jnp
from jax import lax
from jax.sharding import PartitionSpec as P

HEADS = 16
RADIUS = 4
TOK_H = 32


highest = lax.Precision.HIGHEST


def padded(cells, sides, width):
    for axis, dim in sides:
        count = lax.axis_size(axis)
        ends = count - 1
        head = lax.slice_in_dim(cells, 0, width, axis=dim)
        tail = lax.slice_in_dim(cells, cells.shape[dim] - width, cells.shape[dim], axis=dim)
        cells = jnp.concatenate(
            [
                lax.ppermute(tail, axis, [(i, (i + 1) % count) for i in range(ends)]),
                cells,
                lax.ppermute(head, axis, [((i + 1) % count, i) for i in range(ends)]),
            ],
            axis=dim,
        )
    return cells


def normed(stream, gain_row):
    centre = jnp.mean(stream, -1, keepdims=True)
    spread = jnp.mean(jnp.square(stream - centre), -1, keepdims=True)
    return ((stream - centre) * lax.rsqrt(spread + 1e-05) * gain_row).astype(jnp.bfloat16)


def per_device(
    scans, dest, offsets, profile_index, profiles, embed_weight, attn_gain, qkv_weight, out_weight
):
    row_count = lax.axis_size("row")
    col_count = lax.axis_size("col")
    device_count = row_count * col_count
    block_count, strip_rows, channels, tile_cols = scans.shape
    token_cols = tile_cols // 8
    tile_rows = TOK_H * 8
    profile_count = profiles.shape[0]
    model_width = embed_weight.shape[1]
    capacity = max(2, 2 * block_count // device_count)
    slot_count = device_count * capacity
    targets = dest[:, 0]
    position = jnp.arange(block_count, dtype=jnp.int32)
    earlier = (targets[:, None] == targets[None, :]) & (position[:, None] < position[None, :])
    slot_rank = jnp.sum(earlier.astype(jnp.int32), 0)
    slot_index = targets * capacity + slot_rank
    placing = (jnp.arange(slot_count, dtype=jnp.int32)[:, None] == slot_index[None, :]).astype(
        jnp.int32
    )
    slot_source = jnp.sum(placing * (position[None, :] + 1), 1) - 1
    filled = slot_source >= 0
    safe_source = jnp.maximum(slot_source, 0)
    sent_offsets = jnp.where(filled, offsets[safe_source], 0)
    chosen = (profile_index[:, None] == jnp.arange(profile_count, dtype=jnp.int32)[None, :]).astype(
        jnp.float32
    )
    picked = jnp.dot(
        chosen, profiles.reshape(profile_count, strip_rows * tile_cols), precision=highest
    )
    weight_local = picked.reshape(profile_index.shape[0], strip_rows, tile_cols)
    weighted = scans * weight_local[:, :, None, :]
    payload = jnp.where(filled[:, None], weighted.reshape(block_count, -1)[safe_source], 0.0)
    side_data = jnp.where(filled[:, None], weight_local.reshape(block_count, -1)[safe_source], 0.0)
    lead_dims = (device_count, capacity)
    got_payload, got_side, got_offsets = (
        lax.all_to_all(
            payload.reshape(lead_dims + payload.shape[1:]),
            ("row", "col"),
            split_axis=0,
            concat_axis=0,
            tiled=True,
        ),
        lax.all_to_all(
            side_data.reshape(lead_dims + side_data.shape[1:]),
            ("row", "col"),
            split_axis=0,
            concat_axis=0,
            tiled=True,
        ),
        lax.all_to_all(
            sent_offsets.reshape(lead_dims), ("row", "col"), split_axis=0, concat_axis=0, tiled=True
        ),
    )
    got_payload = got_payload.reshape(slot_count, strip_rows, channels, tile_cols)
    got_offsets = got_offsets.reshape(slot_count)
    weight_all = got_side.reshape(slot_count, strip_rows, tile_cols)
    strip_idx = jnp.arange(strip_rows, dtype=jnp.int32)
    landing = (got_offsets[:, None] + strip_idx[None, :]).reshape(slot_count * strip_rows)
    placement = (jnp.arange(tile_rows, dtype=jnp.int32)[:, None] == landing[None, :]).astype(
        jnp.float32
    )
    numerator = jnp.dot(
        placement,
        got_payload.reshape(slot_count * strip_rows, channels * tile_cols),
        precision=highest,
    )
    numerator = numerator.reshape(tile_rows, channels, tile_cols)
    weight_sum = jnp.dot(
        placement, weight_all.reshape(slot_count * strip_rows, tile_cols), precision=highest
    )
    merged = (numerator / (1.0 + weight_sum[:, None, :])).astype(jnp.bfloat16)
    token_count = TOK_H * token_cols
    patches = (
        merged.reshape(TOK_H, 8, channels, token_cols, 8)
        .transpose(0, 3, 2, 1, 4)
        .reshape(token_count, channels * 64)
    )
    stream = jnp.dot(patches, embed_weight, preferred_element_type=jnp.float32)
    head_dim = model_width // HEADS
    score_scale = head_dim ** (-0.5)
    padded_rows = TOK_H + 2 * RADIUS
    padded_cols = token_cols + 2 * RADIUS
    padded_count = padded_rows * padded_cols
    sub_rows = math.gcd(TOK_H, 8)
    sub_cols = math.gcd(token_cols, 8)
    block_rows = TOK_H // sub_rows
    block_cols = token_cols // sub_cols
    block_total = block_rows * block_cols
    win_rows = sub_rows + 2 * RADIUS
    win_cols = sub_cols + 2 * RADIUS
    win_count = win_rows * win_cols
    query_idx = jnp.arange(sub_rows * sub_cols, dtype=jnp.int32)
    query_row = query_idx // sub_cols
    query_col = query_idx % sub_cols
    key_idx = jnp.arange(win_count, dtype=jnp.int32)
    key_row = key_idx // win_cols
    key_col = key_idx % win_cols
    nearby = (jnp.abs(key_row[None, :] - RADIUS - query_row[:, None]) <= RADIUS) & (
        jnp.abs(key_col[None, :] - RADIUS - query_col[:, None]) <= RADIUS
    )
    block_idx = jnp.arange(block_total, dtype=jnp.int32)
    global_row = (
        lax.axis_index("row") * TOK_H
        + (block_idx // block_cols)[:, None] * sub_rows
        + key_row[None, :]
        - RADIUS
    )
    global_col = (
        lax.axis_index("col") * token_cols
        + (block_idx % block_cols)[:, None] * sub_cols
        + key_col[None, :]
        - RADIUS
    )
    inside = (
        (global_row >= 0)
        & (global_row < TOK_H * row_count)
        & (global_col >= 0)
        & (global_col < token_cols * col_count)
    )
    allowed = nearby[None, None, :, :] & inside[:, None, None, :]
    for layer_idx in range(qkv_weight.shape[0]):
        inputs = normed(stream, attn_gain[layer_idx])
        queries = jnp.dot(
            inputs, qkv_weight[layer_idx][:, :model_width], preferred_element_type=jnp.float32
        ).astype(jnp.bfloat16)
        beside_all = padded(
            inputs.reshape(TOK_H, token_cols, model_width), (("row", 0), ("col", 1)), RADIUS
        )
        beside_all = beside_all.reshape(padded_count, model_width)
        keyvals = jnp.dot(
            beside_all, qkv_weight[layer_idx][:, model_width:], preferred_element_type=jnp.float32
        ).astype(jnp.bfloat16)
        keyvals = keyvals.reshape(padded_rows, padded_cols, 2 * model_width)
        windows = jnp.stack(
            [
                keyvals[
                    bi * sub_rows : bi * sub_rows + win_rows,
                    bj * sub_cols : bj * sub_cols + win_cols,
                ]
                for bi in range(block_rows)
                for bj in range(block_cols)
            ]
        )
        windows = windows.reshape(block_total, win_count, 2 * model_width)
        key_heads = windows[:, :, :model_width].reshape(block_total, win_count, HEADS, head_dim)
        values = windows[:, :, model_width:].reshape(block_total, win_count, HEADS, head_dim)
        query_heads = queries.reshape(
            block_rows, sub_rows, block_cols, sub_cols, HEADS, head_dim
        ).transpose(0, 2, 1, 3, 4, 5)
        query_heads = query_heads.reshape(block_total, sub_rows * sub_cols, HEADS, head_dim)
        logits = (
            jnp.einsum(
                "bqhd,bkhd->bhqk", query_heads, key_heads, preferred_element_type=jnp.float32
            )
            * score_scale
        )
        logits = jnp.where(allowed, logits, -1e30)
        row_max = jnp.max(logits, -1, keepdims=True)
        exponent = jnp.exp(logits - row_max)
        attention = (exponent / jnp.sum(exponent, -1, keepdims=True)).astype(jnp.bfloat16)
        attended = jnp.einsum(
            "bhqk,bkhd->bqhd", attention, values, preferred_element_type=jnp.float32
        )
        attended = attended.astype(jnp.bfloat16).reshape(
            block_rows, block_cols, sub_rows, sub_cols, model_width
        )
        attended = attended.transpose(0, 2, 1, 3, 4).reshape(token_count, model_width)
        stream = stream + jnp.dot(
            attended, out_weight[layer_idx], preferred_element_type=jnp.float32
        )
    return stream.astype(jnp.bfloat16).reshape(TOK_H, token_cols, model_width)


def solution(mesh):
    placed = (
        P(("row", "col"), None, None, None),
        P(("row", "col"), None),
        P(("row", "col")),
        P(("row", "col")),
        P(),
        P(),
        P(),
        P(),
        P(),
    )
    return jax.shard_map(
        per_device, mesh=mesh, in_specs=placed, out_specs=P("row", "col", None), check_vma=False
    )
```

profile of v0, /device:TPU:20, one launch (start us, length us, event | category | flops | bytes accessed | tf_op | source)
XLA Modules:
  0.0 368.8 jit_solution(16816035063951867314)
XLA Ops:
  4.3 5.9 %all-to-all-start = ((s32[32,1,8]{2,1,0:T(1,128)}), s32[32,1,8]{2,1,0:T(1,128)S(1)}, u32[]{:S(2)}, u32[]{:S(2)}) async-start(s32[32,1,8]{2,1,0:T(1,128)} %bitcast.1), calls=%async_computation | async-start | bytes 32768 | tf_op jit(solution)/shard_map/all_to_all | solution.py:90
  16.8 3.8 %gather_fusion.1 = f32[256,4096]{1,0:T(8,128)} fusion(f32[128,4096]{1,0:T(8,128)S(1)} %bitcast.111, s32[1024]{0:T(1024)S(1)} %pad_clamp_fusion), kind=kCustom, calls=%fused_computation.1 | custom fusion | bytes 8389632 | tf_op jit(solution)/shard_map/gather | solution.py:72
  20.7 5.8 %all-to-all-start.2 = ((f32[32,8,512]{2,1,0:T(8,128)}), f32[32,8,512]{2,1,0:T(8,128)S(1)}, u32[]{:S(2)}, u32[]{:S(2)}) async-start(f32[32,8,512]{2,1,0:T(8,128)} %bitcast_select_fusion.1), calls=%async_computation.2 | async-start | bytes 1048576 | tf_op jit(solution)/shard_map/all_to_all | solution.py:83
  26.5 4.8 %bitcast_select_fusion = f32[32,8,4096]{2,1,0:T(8,128)} fusion(f32[256,4096]{1,0:T(8,128)} %gather_fusion.1, pred[32,8]{1,0:T(8,128)(4,1)S(1)} %ge.34), kind=kLoop, calls=%fused_computation.19 | loop fusion | flops 1048576 | bytes 8388864 | tf_op jit(solution)/shard_map/jit(_where)/select_n | solution.py:72
  31.3 7.9 %all-to-all-done.2 = f32[32,8,512]{2,1,0:T(8,128)S(1)} async-done(((f32[32,8,512]{2,1,0:T(8,128)}), f32[32,8,512]{2,1,0:T(8,128)S(1)}, u32[]{:S(2)}, u32[]{:S(2)}) %all-to-all-start.2) | async-done | bytes 524320 | tf_op jit(solution)/shard_map/all_to_all | solution.py:83
  39.2 6.9 %all-to-all-start.1 = ((f32[32,8,4096]{2,1,0:T(8,128)}), f32[32,8,4096]{2,1,0:T(8,128)}, u32[]{:S(2)}, u32[]{:S(2)}) async-start(f32[32,8,4096]{2,1,0:T(8,128)} %bitcast_select_fusion), calls=%async_computation.1 | async-start | bytes 8388608 | tf_op jit(solution)/shard_map/all_to_all | solution.py:76
  47.5 10.5 %slice_bitcast_fusion = (bf16[1024,3072]{1,0:T(8,128)(2,1)}, bf16[1024,3072]{1,0:T(8,128)(2,1)}) fusion(bf16[2,1024,3072]{2,1,0:T(8,128)(2,1)} %param.16), kind=kLoop, calls=%fused_computation.13 | loop fusion | bytes 25165824 | tf_op jit(solution)/shard_map/squeeze | solution.py:171
  60.3 76.2 %all-to-all-done.1 = f32[32,8,4096]{2,1,0:T(8,128)} async-done(((f32[32,8,4096]{2,1,0:T(8,128)}), f32[32,8,4096]{2,1,0:T(8,128)}, u32[]{:S(2)}, u32[]{:S(2)}) %all-to-all-start.1) | async-done | bytes 4194336 | tf_op jit(solution)/shard_map/all_to_all | solution.py:76
  136.4 5.3 %reshape_reshape.6 = f32[1024,1024]{1,0:T(8,128)} reshape(f32[32,8,4096]{2,1,0:T(8,128)} %all-to-all-done.1) | data formatting | bytes 8388608 | tf_op jit(solution)/shard_map/reshape;reshape | solution.py:104
  141.7 5.3 %copy.80 = f32[1024,1024]{1,0:T(8,128)} copy(f32[1024,1024]{0,1:T(8,128)} %bitcast.115) | data formatting | bytes 8388608 | tf_op jit(solution)/shard_map/dot_general | solution.py:102
  147.0 4.5 %fusion.43 = bf16[256,8,128]{2,0,1:T(8,128)(2,1)S(1)} fusion(f32[8,128,1024]{2,1,0:T(8,128)} %bitcast.141, f32[256,128]{1,0:T(8,128)S(1)} %convolution_add_fusion, s32[1024]{0:T(1024)S(1)} %add.232), kind=kOutput, calls=%fused_computation.54 | convolution fusion | flops 3222011904 | bytes 4853760 | tf_op jit(solution)/shard_map/dot_general | solution.py:102
  151.9 10.6 %reshape.445 = bf16[32,8,8,16,8]{4,3,2,1,0:T(8,128)(2,1)} reshape(bf16[256,8,128]{2,1,0:T(8,128)(2,1)S(1)} %copy.81) | data formatting | bytes 1048576 | tf_op jit(solution)/shard_map/reshape | solution.py:114
  162.5 10.6 %copy.82 = bf16[32,16,8,8,8]{1,0,4,3,2:T(8,128)(2,1)} copy(bf16[32,16,8,8,8]{4,1,2,3,0:T(8,128)(2,1)} %bitcast.112) | data formatting | bytes 1048576 | tf_op jit(solution)/shard_map/transpose | solution.py:115
  173.1 8.4 %reshape.446 = bf16[512,512]{0,1:T(8,128)(2,1)} reshape(bf16[32,16,8,8,8]{1,0,4,3,2:T(8,128)(2,1)} %copy.82) | data formatting | bytes 1048576 | tf_op jit(solution)/shard_map/reshape | solution.py:116
  184.1 2.3 collective-permute-start.1
  186.5 3.5 collective-permute-start
  191.5 3.4 collective-permute-done
  197.9 4.5 %collective-permute-start.3 = (bf16[40,4,1024]{2,1,0:T(4,128)(2,1)}, bf16[40,4,1024]{2,1,0:T(4,128)(2,1)}, u32[]{:S(2)}, u32[]{:S(2)}) collective-permute-start(bf16[40,4,1024]{2,1,0:T(4,128)(2,1)} %get-tuple-element.32), channel_id=1, source_target_pairs={{1,0},{2,1},{3,2},{4,3},{5,4},{6,5},{7,6},{9,8},{10,9},{11,10},{12... | collective-permute-start | bytes 983048 | tf_op jit(solution)/shard_map/ppermute | solution.py:26
  202.4 3.8 %fusion.35 = bf16[512,1024]{1,0:T(8,128)(2,1)} fusion(bf16[512,1024]{1,0:T(8,128)(2,1)S(1)} %multiply_convert_fusion.1, bf16[1024,3072]{1,0:T(8,128)(2,1)} %get-tuple-element.8), kind=kOutput, calls=%fused_computation.51 | convolution fusion | flops 1074266112 | bytes 4194304 | tf_op jit(solution)/shard_map/dot_general | solution.py:163
  206.2 4.5 %reshape.451 = bf16[4,8,2,8,16,64]{5,4,3,2,1,0:T(8,128)(2,1)} reshape(bf16[512,1024]{1,0:T(8,128)(2,1)} %fusion.35) | data formatting | bytes 2097152 | tf_op jit(solution)/shard_map/reshape | solution.py:187
  210.7 3.5 copy.91
  216.4 6.7 %fusion.16 = bf16[960,2048]{1,0:T(8,128)(2,1)S(1)} fusion(bf16[960,1024]{1,0:T(8,128)(2,1)S(1)} %bitcast.148, bf16[1024,3072]{1,0:T(8,128)(2,1)} %get-tuple-element.8), kind=kOutput, calls=%fused_computation.28 | convolution fusion | flops 4028497920 | bytes 10092544 | tf_op jit(solution)/shard_map/dot_general | solution.py:170
  223.1 3.0 fusion.78
  228.4 2.3 copy.89
  232.9 2.3 copy.87
  235.2 2.3 copy.86
  237.5 2.3 copy.85
  247.8 3.5 fusion.76
  251.4 8.5 %fusion.83 = (f32[8,16,64]{2,1,0:T(8,128)S(1)}, f32[8,16,64,256]{3,2,1,0:T(8,128)}) fusion(pred[8,64,256]{2,1,0:T(8,128)(4,1)S(1)} %broadcast_and_fusion, bf16[8,64,16,64]{3,1,2,0:T(8,128)(2,1)} %bitcast.147, bf16[8,256,16,64]{1,3,2,0:T(8,128)(2,1)} %bitcast.145), kind=kOutput, calls=%fused_computation.155 | convolution fusion | flops 276824320 | bytes 13795328 | tf_op jit(solution)/shard_map/sub | solution.py:199
  259.9 7.3 %convert_bitcast_fusion.1 = bf16[8,64,16,64]{1,3,2,0:T(8,128)(2,1)} fusion(bf16[8,256,16,64]{1,3,2,0:T(8,128)(2,1)} %bitcast.143, f32[8,16,64,256]{3,2,1,0:T(8,128)} %get-tuple-element.42, f32[8,16,64]{2,1,0:T(8,128)S(1)} %get-tuple-element.41), kind=kOutput, calls=%fused_computation.45 | convolution fusion | flops 273154048 | bytes 13664256 | tf_op jit(solution)/shard_map/bhqk,bkhd->bqhd/dot_general | solution.py:201
  267.2 4.4 %copy.92 = bf16[8,64,16,64]{3,2,1,0:T(8,128)(2,1)} copy(bf16[8,64,16,64]{1,3,2,0:T(8,128)(2,1)} %convert_bitcast_fusion.1) | data formatting | bytes 2097152 | tf_op jit(solution)/shard_map/convert_element_type | solution.py:204
  271.6 3.2 reshape.454
  275.0 2.9 fusion.84
  279.6 3.9 %collective-permute-start.5 = (bf16[4,16,1024]{2,1,0:T(8,128)(2,1)S(1)}, bf16[4,16,1024]{2,1,0:T(8,128)(2,1)S(1)}, u32[]{:S(2)}, u32[]{:S(2)}) collective-permute-start(bf16[4,16,1024]{2,1,0:T(8,128)(2,1)S(1)} %bitcast.155), channel_id=1, source_target_pairs={{8,0},{16,8},{24,16},{9,1},{17,9},{25,17},{10,2},{18,10},{26,18},{... | collective-permute-start | bytes 393224 | tf_op jit(solution)/shard_map/ppermute | solution.py:26
  286.5 3.9 %collective-permute-done.4 = bf16[4,16,1024]{2,1,0:T(8,128)(2,1)S(1)} collective-permute-done((bf16[4,16,1024]{2,1,0:T(8,128)(2,1)S(1)}, bf16[4,16,1024]{2,1,0:T(8,128)(2,1)S(1)}, u32[]{:S(2)}, u32[]{:S(2)}) %collective-permute-start.4) | collective-permute-done | bytes 131104 | tf_op jit(solution)/shard_map/ppermute | solution.py:24
  293.4 4.5 %collective-permute-start.7 = (bf16[40,4,1024]{2,1,0:T(4,128)(2,1)}, bf16[40,4,1024]{2,1,0:T(4,128)(2,1)}, u32[]{:S(2)}, u32[]{:S(2)}) collective-permute-start(bf16[40,4,1024]{2,1,0:T(4,128)(2,1)} %get-tuple-element.30), channel_id=1, source_target_pairs={{1,0},{2,1},{3,2},{4,3},{5,4},{6,5},{7,6},{9,8},{10,9},{11,10},{12... | collective-permute-start | bytes 983048 | tf_op jit(solution)/shard_map/ppermute | solution.py:26
  298.0 3.8 %fusion.38 = bf16[512,1024]{1,0:T(8,128)(2,1)} fusion(bf16[512,1024]{1,0:T(8,128)(2,1)S(1)} %multiply_convert_fusion, bf16[1024,3072]{1,0:T(8,128)(2,1)} %get-tuple-element.7), kind=kOutput, calls=%fused_computation.52 | convolution fusion | flops 1074266112 | bytes 4194304 | tf_op jit(solution)/shard_map/dot_general | solution.py:163
  301.8 3.1 reshape.460
  309.0 6.7 %fusion.19 = bf16[960,2048]{1,0:T(8,128)(2,1)S(1)} fusion(bf16[960,1024]{1,0:T(8,128)(2,1)S(1)} %bitcast.149, bf16[1024,3072]{1,0:T(8,128)(2,1)} %get-tuple-element.7), kind=kOutput, calls=%fused_computation.29 | convolution fusion | flops 4028497920 | bytes 10092544 | tf_op jit(solution)/shard_map/dot_general | solution.py:170
  315.6 2.4 fusion.77
  324.8 2.3 copy.98
  327.1 2.3 copy.97
  337.8 3.5 fusion.75
  341.3 7.9 %fusion.85 = (f32[8,16,64]{2,1,0:T(8,128)S(1)}, f32[8,16,64,256]{3,2,1,0:T(8,128)}) fusion(pred[8,64,256]{2,1,0:T(8,128)(4,1)S(1)} %broadcast_and_fusion, bf16[8,64,16,64]{3,1,2,0:T(8,128)(2,1)S(1)} %bitcast.146, bf16[8,256,16,64]{1,3,2,0:T(8,128)(2,1)} %bitcast.144), kind=kOutput, calls=%fused_computation.157 | convolution fusion | flops 276824320 | bytes 13795328 | tf_op jit(solution)/shard_map/sub | solution.py:199
  349.2 7.4 %convert_bitcast_fusion = bf16[8,64,16,64]{1,3,2,0:T(8,128)(2,1)} fusion(bf16[8,256,16,64]{1,3,2,0:T(8,128)(2,1)} %bitcast.142, f32[8,16,64,256]{3,2,1,0:T(8,128)} %get-tuple-element.46, f32[8,16,64]{2,1,0:T(8,128)S(1)} %get-tuple-element.45), kind=kOutput, calls=%fused_computation.41 | convolution fusion | flops 273154048 | bytes 13664256 | tf_op jit(solution)/shard_map/bhqk,bkhd->bqhd/dot_general | solution.py:201
  356.6 4.7 %copy.103 = bf16[8,64,16,64]{3,2,1,0:T(8,128)(2,1)} copy(bf16[8,64,16,64]{1,3,2,0:T(8,128)(2,1)} %convert_bitcast_fusion) | data formatting | bytes 2097152 | tf_op jit(solution)/shard_map/convert_element_type | solution.py:204
  361.3 3.2 reshape.463
  364.6 3.9 %add_convert_fusion = bf16[512,1024]{1,0:T(8,128)(2,1)} fusion(f32[512,1024]{1,0:T(8,128)S(1)} %copy-done.3, bf16[512,1024]{1,0:T(8,128)(2,1)S(1)} %bitcast.151, bf16[2,1024,1024]{2,1,0:T(8,128)(2,1)} %param.17), kind=kOutput, calls=%fused_computation.39 | convolution fusion | flops 1074790400 | bytes 6291456 | tf_op jit(solution)/shard_map/dot_general | solution.py:208
  (125 shorter events, 63.5 us)
Async XLA Ops:
  0.0 181.5 %copy-start = (bf16[512,1024]{1,0:T(8,128)(2,1)S(1)}, bf16[512,1024]{1,0:T(8,128)(2,1)}, u32[]{:S(2)}) copy-start(bf16[512,1024]{1,0:T(8,128)(2,1)} %param.14) | copy-start | bytes 3145732
  4.3 16.4 %all-to-all-start = ((s32[32,1,8]{2,1,0:T(1,128)}), s32[32,1,8]{2,1,0:T(1,128)S(1)}, u32[]{:S(2)}, u32[]{:S(2)}) async-start(s32[32,1,8]{2,1,0:T(1,128)} %bitcast.1), calls=%async_computation | async-start | bytes 32768 | tf_op jit(solution)/shard_map/all_to_all | solution.py:90
  20.7 18.5 %all-to-all-start.2 = ((f32[32,8,512]{2,1,0:T(8,128)}), f32[32,8,512]{2,1,0:T(8,128)S(1)}, u32[]{:S(2)}, u32[]{:S(2)}) async-start(f32[32,8,512]{2,1,0:T(8,128)} %bitcast_select_fusion.1), calls=%async_computation.2 | async-start | bytes 1048576 | tf_op jit(solution)/shard_map/all_to_all | solution.py:83
  31.3 15.5 %copy-start.19 = (f32[2,1024]{1,0:T(2,128)S(1)}, f32[2,1024]{1,0:T(2,128)}, u32[]{:S(2)}) copy-start(f32[2,1024]{1,0:T(2,128)} %param.15) | copy-start | bytes 24580
  39.2 97.2 %all-to-all-start.1 = ((f32[32,8,4096]{2,1,0:T(8,128)}), f32[32,8,4096]{2,1,0:T(8,128)}, u32[]{:S(2)}, u32[]{:S(2)}) async-start(f32[32,8,4096]{2,1,0:T(8,128)} %bitcast_select_fusion), calls=%async_computation.1 | async-start | bytes 8388608 | tf_op jit(solution)/shard_map/all_to_all | solution.py:76
  181.5 8.5 %copy-start.18 = (pred[8,256]{1,0:T(8,128)(4,1)S(1)}, pred[8,256]{1,0:T(8,128)(4,1)}, u32[]{:S(2)}) copy-start(pred[8,256]{1,0:T(8,128)(4,1)} %fusion.64) | copy-start | bytes 6148
  184.1 7.3 %collective-permute-start.1 = (bf16[4,16,1024]{2,1,0:T(8,128)(2,1)S(1)}, bf16[4,16,1024]{2,1,0:T(8,128)(2,1)S(1)}, u32[]{:S(2)}, u32[]{:S(2)}) collective-permute-start(bf16[4,16,1024]{2,1,0:T(8,128)(2,1)S(1)} %bitcast.153), channel_id=1, source_target_pairs={{8,0},{16,8},{24,16},{9,1},{17,9},{25,17},{10,2},{18,10},{26,18},{... | collective-permute-start | bytes 393224 | tf_op jit(solution)/shard_map/ppermute | solution.py:26
  186.5 8.4 %collective-permute-start = (bf16[4,16,1024]{2,1,0:T(8,128)(2,1)S(1)}, bf16[4,16,1024]{2,1,0:T(8,128)(2,1)S(1)}, u32[]{:S(2)}, u32[]{:S(2)}) collective-permute-start(bf16[4,16,1024]{2,1,0:T(8,128)(2,1)S(1)} %bitcast.152), channel_id=1, source_target_pairs={{0,8},{8,16},{16,24},{1,9},{9,17},{17,25},{2,10},{10,18},{18,26},{... | collective-permute-start | bytes 393224 | tf_op jit(solution)/shard_map/ppermute | solution.py:24
  196.0 18.3 %collective-permute-start.2 = (bf16[40,4,1024]{2,1,0:T(4,128)(2,1)}, bf16[40,4,1024]{2,1,0:T(4,128)(2,1)}, u32[]{:S(2)}, u32[]{:S(2)}) collective-permute-start(bf16[40,4,1024]{2,1,0:T(4,128)(2,1)} %get-tuple-element.31), channel_id=1, source_target_pairs={{0,1},{1,2},{2,3},{3,4},{4,5},{5,6},{6,7},{8,9},{9,10},{10,11},{11... | collective-permute-start | bytes 983048 | tf_op jit(solution)/shard_map/ppermute | solution.py:24
  197.9 16.4 %collective-permute-start.3 = (bf16[40,4,1024]{2,1,0:T(4,128)(2,1)}, bf16[40,4,1024]{2,1,0:T(4,128)(2,1)}, u32[]{:S(2)}, u32[]{:S(2)}) collective-permute-start(bf16[40,4,1024]{2,1,0:T(4,128)(2,1)} %get-tuple-element.32), channel_id=1, source_target_pairs={{1,0},{2,1},{3,2},{4,3},{5,4},{6,5},{7,6},{9,8},{10,9},{11,10},{12... | collective-permute-start | bytes 983048 | tf_op jit(solution)/shard_map/ppermute | solution.py:26
  243.3 2.8 copy-start.14
  243.3 2.9 copy-start.12
  243.3 3.0 copy-start.10
  244.8 1.7 copy-start.8
  246.2 1.3 copy-start.6
  246.3 1.5 copy-start.4
  274.9 4.3 %copy-start.17 = (f32[1,1024]{1,0:T(1,128)S(1)}, f32[1,1024]{1,0:T(1,128)}, u32[]{:S(2)}) copy-start(f32[1,1024]{1,0:T(1,128)} %get-tuple-element.37) | copy-start | bytes 12292
  277.9 1.3 copy-start.2
  279.6 6.9 %collective-permute-start.5 = (bf16[4,16,1024]{2,1,0:T(8,128)(2,1)S(1)}, bf16[4,16,1024]{2,1,0:T(8,128)(2,1)S(1)}, u32[]{:S(2)}, u32[]{:S(2)}) collective-permute-start(bf16[4,16,1024]{2,1,0:T(8,128)(2,1)S(1)} %bitcast.155), channel_id=1, source_target_pairs={{8,0},{16,8},{24,16},{9,1},{17,9},{25,17},{10,2},{18,10},{26,18},{... | collective-permute-start | bytes 393224 | tf_op jit(solution)/shard_map/ppermute | solution.py:26
  283.5 6.9 %collective-permute-start.4 = (bf16[4,16,1024]{2,1,0:T(8,128)(2,1)S(1)}, bf16[4,16,1024]{2,1,0:T(8,128)(2,1)S(1)}, u32[]{:S(2)}, u32[]{:S(2)}) collective-permute-start(bf16[4,16,1024]{2,1,0:T(8,128)(2,1)S(1)} %bitcast.154), channel_id=1, source_target_pairs={{0,8},{8,16},{16,24},{1,9},{9,17},{17,25},{2,10},{10,18},{18,26},{... | collective-permute-start | bytes 393224 | tf_op jit(solution)/shard_map/ppermute | solution.py:24
  291.5 15.3 %collective-permute-start.6 = (bf16[40,4,1024]{2,1,0:T(4,128)(2,1)}, bf16[40,4,1024]{2,1,0:T(4,128)(2,1)}, u32[]{:S(2)}, u32[]{:S(2)}) collective-permute-start(bf16[40,4,1024]{2,1,0:T(4,128)(2,1)} %get-tuple-element.29), channel_id=1, source_target_pairs={{0,1},{1,2},{2,3},{3,4},{4,5},{5,6},{6,7},{8,9},{9,10},{10,11},{11... | collective-permute-start | bytes 983048 | tf_op jit(solution)/shard_map/ppermute | solution.py:24
  293.4 13.4 %collective-permute-start.7 = (bf16[40,4,1024]{2,1,0:T(4,128)(2,1)}, bf16[40,4,1024]{2,1,0:T(4,128)(2,1)}, u32[]{:S(2)}, u32[]{:S(2)}) collective-permute-start(bf16[40,4,1024]{2,1,0:T(4,128)(2,1)} %get-tuple-element.30), channel_id=1, source_target_pairs={{1,0},{2,1},{3,2},{4,3},{5,4},{6,5},{7,6},{9,8},{10,9},{11,10},{12... | collective-permute-start | bytes 983048 | tf_op jit(solution)/shard_map/ppermute | solution.py:26
  330.7 5.4 %copy-start.15 = (bf16[1,256,2048]{1,2,0:T(8,128)(2,1)S(1)}, bf16[1,256,2048]{1,2,0:T(8,128)(2,1)}, u32[]{:S(2)}) copy-start(bf16[1,256,2048]{1,2,0:T(8,128)(2,1)} %copy.96) | copy-start | bytes 3145732
  332.0 4.2 %copy-start.13 = (bf16[1,256,2048]{1,2,0:T(8,128)(2,1)S(1)}, bf16[1,256,2048]{1,2,0:T(8,128)(2,1)}, u32[]{:S(2)}) copy-start(bf16[1,256,2048]{1,2,0:T(8,128)(2,1)} %copy.97) | copy-start | bytes 3145732
  333.4 3.0 copy-start.11
  334.7 1.7 copy-start.9
  336.1 1.3 copy-start.7
  336.2 1.5 copy-start.5
  337.8 3.6 copy-start.16
  356.6 8.0 %copy-start.3 = (f32[512,1024]{1,0:T(8,128)S(1)}, f32[512,1024]{1,0:T(8,128)}, u32[]{:S(2)}) copy-start(f32[512,1024]{1,0:T(8,128)} %copy-done.2) | copy-start | bytes 6291460
  364.6 3.9 %copy-start.1 = (bf16[512,1024]{1,0:T(8,128)(2,1)S(1)}, bf16[512,1024]{1,0:T(8,128)(2,1)}, u32[]{:S(2)}) copy-start(bf16[512,1024]{1,0:T(8,128)(2,1)} %param.14) | copy-start | bytes 3145732
where the time goes:
time: 376 us; the launch traced here: 369 us
  local copies, waits for them, and re-layouts  145 us (39%)
  waiting for transfers between devices  93.8 us (25%)
  matrix products  67 us (18%)
  starting transfers between devices  43.2 us (11%)
  other arithmetic  18.8 us (5%)
    all_to_all x1, waiting for transfers between devices, per_device(): lax.all_to_all(payload.reshape(lead_dims + payload.shape[1:]), ('row', 'c...  76.2 us
    another operation x18, local copies, waits for them, and re-layouts, per_device(): jnp.stack([keyvals[bi * sub_rows:bi * sub_rows + win_rows, bj * sub_cols:...  32.6 us
    sub x2, matrix products, per_device(): exponent = jnp.exp(logits - row_max)  16.4 us
    ppermute x4, starting transfers between devices, padded(): lax.ppermute(head, axis, [((i + 1) % count, i) for i in range(ends)])  15.3 us
    dot_general x2, matrix products, per_device(): jnp.einsum('bhqk,bkhd->bqhd', attention, values, preferred_element_type=j...  14.7 us
    dot_general x2, matrix products, per_device(): jnp.dot(beside_all, qkv_weight[layer_idx][:, model_width:], preferred_ele...  13.3 us
    unnamed x55, local copies, waits for them, and re-layouts  11.3 us
    transpose x1, local copies, waits for them, and re-layouts, per_device(): patches = merged.reshape(TOK_H, 8, channels, token_cols, 8).transpose(0,...  10.6 us
  transfers between devices with their start and end apart: 11, of which 6 were waited for; matrix products, arithmetic and copies ran while one was open for 14% of the time, Pallas kernels for 0%

commit v1 on v0

v1 whole, which is shorter than its diff:
```python
import functools

import jax
import jax.numpy as jnp
from jax import lax
from jax.experimental import pallas as pl
from jax.experimental.pallas import tpu as pltpu
from jax.sharding import PartitionSpec as P

HEADS = 16
RADIUS = 4
TOK_H = 32
PATCH = 8
BAND = 8

VMEM = pl.BlockSpec(memory_space=pltpu.VMEM)
SMEM = pl.BlockSpec(memory_space=pltpu.SMEM)


def place_kernel(capacity, empty, dest, offsets, profile, scans, payload, meta, count):
    blocks = scans.shape[0]
    slots = payload.shape[0]
    payload[...] = jnp.zeros_like(payload)

    def clear_slot(i, c):
        meta[i] = empty
        return c

    def clear_count(i, c):
        count[i] = 0
        return c

    lax.fori_loop(0, slots, clear_slot, 0, unroll=8)
    lax.fori_loop(0, slots // capacity, clear_count, 0, unroll=8)

    def put(b, c):
        tile = dest[b]
        rank = count[tile]
        count[tile] = rank + 1
        slot = tile * capacity + rank
        meta[slot] = profile[b] * 256 + offsets[b]
        payload[slot] = scans[b].astype(jnp.bfloat16)
        return c

    lax.fori_loop(0, blocks, put, 0, unroll=4)


def normed(stream, gain_row):
    centre = jnp.mean(stream, -1, keepdims=True)
    spread = jnp.mean(jnp.square(stream - centre), -1, keepdims=True)
    return ((stream - centre) * lax.rsqrt(spread + 1e-05) * gain_row).astype(jnp.bfloat16)


def merge_kernel(meta, got, weights, embed, gain, stream, inputs, num, den, turned):
    slots = got.shape[0]
    rows = got.shape[1]
    lanes = got.shape[2]
    num[...] = jnp.zeros_like(num)
    den[...] = jnp.ones_like(den)

    def add(s, c):
        m = meta[s]
        w = weights[m // 256]
        at = pl.ds(pl.multiple_of((m % 256) * 8, 8), rows)
        num[at, :] += got[s].astype(jnp.float32) * w
        den[at, :] += w
        return c

    lax.fori_loop(0, slots, add, 0, unroll=4)
    group = PATCH * 8

    def turn(i, c):
        at = pl.ds(pl.multiple_of(i * group, group), group)
        merged = (num[at, :] / den[at, :]).astype(jnp.bfloat16).astype(jnp.float32)
        turned[pl.ds(pl.multiple_of(i * lanes, lanes), lanes), :] = merged.T
        return c

    lax.fori_loop(0, TOK_H, turn, 0, unroll=4)
    part = 128

    def embed_part(k, c):
        total = None
        for q in range(PATCH):
            lhs = turned[pl.ds(k * part * PATCH + q, part, stride=PATCH), :]
            term = jnp.dot(
                lhs.astype(jnp.bfloat16), embed[q], preferred_element_type=jnp.float32
            )
            total = term if total is None else total + term
        at = pl.ds(pl.multiple_of(k * part, part), part)
        stream[at, :] = total
        inputs[at, :] = normed(total, gain[...])
        return c

    lax.fori_loop(0, stream.shape[0] // part, embed_part, 0)


def layer_kernel(
    last, token_cols, centre, side, qkv, out_w, stream, bias, gain, *refs
):
    if last:
        tokens, q_ref, kc, ks = refs
    else:
        new_stream, inputs, q_ref, kc, ks = refs
    width = out_w.shape[0]
    head_dim = width // HEADS
    count = stream.shape[0]
    top = RADIUS * token_cols
    step = 512

    def project(n, c):
        cols = pl.ds(pl.multiple_of(n * step, step), step)
        q_ref[:, cols] = (
            jnp.dot(
                centre[top : top + count, :], qkv[:, cols], preferred_element_type=jnp.float32
            ).astype(jnp.bfloat16)
            * head_dim ** (-0.5)
        ).astype(jnp.bfloat16)
        return c

    def project_kv(n, c):
        cols = pl.ds(pl.multiple_of(n * step, step), step)
        from_cols = pl.ds(pl.multiple_of(width + n * step, step), step)
        w = qkv[:, from_cols]
        kc[:, cols] = jnp.dot(centre[...], w, preferred_element_type=jnp.float32).astype(
            jnp.bfloat16
        )
        ks[:, cols] = jnp.dot(side[...], w, preferred_element_type=jnp.float32).astype(
            jnp.bfloat16
        )
        return c

    lax.fori_loop(0, width // step, project, 0)
    lax.fori_loop(0, 2 * width // step, project_kv, 0)
    queries = BAND * token_cols
    c_keys = (BAND + 2 * RADIUS) * token_cols
    s_keys = (BAND + 2 * RADIUS) * 2 * RADIUS
    pair = 2 * head_dim
    low = lax.broadcasted_iota(jnp.int32, (queries, pair), 1) < head_dim

    def band(b, carry):
        q_at = pl.ds(pl.multiple_of(b * queries, queries), queries)
        c_at = pl.ds(pl.multiple_of(b * queries, queries), c_keys)
        s_at = pl.ds(pl.multiple_of(b * BAND * 2 * RADIUS, BAND * 2 * RADIUS), s_keys)
        band_bias = bias[b]
        both = jnp.concatenate([band_bias, band_bias], 0)
        ones = jnp.ones((c_keys + s_keys, pair), jnp.bfloat16)
        pieces = []
        for h in range(HEADS // 2):
            cols = slice(h * pair, (h + 1) * pair)
            v_cols = slice(width + h * pair, width + (h + 1) * pair)
            q = q_ref[q_at, cols]
            zero = jnp.zeros_like(q)
            q2 = jnp.concatenate([jnp.where(low, q, zero), jnp.where(low, zero, q)], 0)
            k = jnp.concatenate([kc[c_at, cols], ks[s_at, cols]], 0)
            v = jnp.concatenate([kc[c_at, v_cols], ks[s_at, v_cols]], 0)
            logits = lax.dot_general(
                q2, k, (((1,), (1,)), ((), ())), preferred_element_type=jnp.float32
            )
            logits = logits + both
            top_logit = jnp.max(logits, -1, keepdims=True)
            weight = jnp.exp(logits - top_logit).astype(jnp.bfloat16)
            summed = jnp.dot(
                weight, jnp.concatenate([v, ones], 1), preferred_element_type=jnp.float32
            )
            share = summed[:, :pair] / summed[:, pair:]
            pieces.append(jnp.where(low, share[:queries], share[queries:]).astype(jnp.bfloat16))
        attended = jnp.concatenate(pieces, 1)
        total = stream[q_at, :] + jnp.dot(
            attended, out_w[...], preferred_element_type=jnp.float32
        )
        if last:
            tokens[q_at, :] = total.astype(jnp.bfloat16)
        else:
            new_stream[q_at, :] = total
            inputs[q_at, :] = normed(total, gain[...])
        return carry

    lax.fori_loop(0, count // queries, band, 0)


def shifted(cells, axis, up):
    count = lax.axis_size(axis)
    pairs = [(i, i + 1) if up else (i + 1, i) for i in range(count - 1)]
    return lax.ppermute(cells, axis, pairs)


def surround(inputs, token_cols):
    width = inputs.shape[-1]
    cells = inputs.reshape(TOK_H, token_cols, width)
    centre = jnp.concatenate(
        [
            shifted(cells[TOK_H - RADIUS :], "row", True),
            cells,
            shifted(cells[:RADIUS], "row", False),
        ],
        0,
    )
    side = jnp.concatenate(
        [
            shifted(centre[:, token_cols - RADIUS :], "col", True),
            shifted(centre[:, :RADIUS], "col", False),
        ],
        1,
    )
    return centre.reshape(-1, width), side.reshape(-1, width)


def window_bias(token_cols):
    bands = TOK_H // BAND
    win = BAND + 2 * RADIUS
    q = jnp.arange(BAND * token_cols, dtype=jnp.int32)
    q_row, q_col = q // token_cols, q % token_cols
    c = jnp.arange(win * token_cols, dtype=jnp.int32)
    s = jnp.arange(win * 2 * RADIUS, dtype=jnp.int32)
    s_off = s % (2 * RADIUS)
    k_row = jnp.concatenate([c // token_cols, s // (2 * RADIUS)]) - RADIUS
    k_col = jnp.concatenate(
        [c % token_cols, jnp.where(s_off < RADIUS, s_off - RADIUS, token_cols + s_off - RADIUS)]
    )
    near = (jnp.abs(k_row[None] - q_row[:, None]) <= RADIUS) & (
        jnp.abs(k_col[None] - q_col[:, None]) <= RADIUS
    )
    g_row = (
        lax.axis_index("row") * TOK_H
        + jnp.arange(bands, dtype=jnp.int32)[:, None] * BAND
        + k_row[None]
    )
    g_col = lax.axis_index("col") * token_cols + k_col
    inside = (
        (g_row >= 0)
        & (g_row < TOK_H * lax.axis_size("row"))
        & (g_col >= 0)[None]
        & (g_col < token_cols * lax.axis_size("col"))[None]
    )
    return jnp.where(near[None] & inside[:, None, :], 0.0, -1e30).astype(jnp.float32)


def per_device(
    scans, dest, offsets, profile_index, profiles, embed_weight, attn_gain, qkv_weight, out_weight
):
    device_count = lax.axis_size("row") * lax.axis_size("col")
    blocks, strip_rows, channels, tile_cols = scans.shape
    token_cols = tile_cols // PATCH
    count = TOK_H * token_cols
    tile_rows = TOK_H * PATCH
    profile_count = profiles.shape[0]
    width = embed_weight.shape[1]
    layers = qkv_weight.shape[0]
    capacity = max(2, 2 * blocks // device_count)
    slots = device_count * capacity
    rows = strip_rows * channels
    f32, bf16 = jnp.float32, jnp.bfloat16
    params = pltpu.CompilerParams(vmem_limit_bytes=56 * 2**20)

    payload, meta = pl.pallas_call(
        functools.partial(place_kernel, capacity, profile_count * 256),
        out_shape=(
            jax.ShapeDtypeStruct((slots, rows, tile_cols), bf16),
            jax.ShapeDtypeStruct((slots,), jnp.int32),
        ),
        in_specs=[SMEM, SMEM, SMEM, VMEM],
        out_specs=(VMEM, SMEM),
        scratch_shapes=[pltpu.SMEM((device_count,), jnp.int32)],
        compiler_params=params,
        name="place",
    )(dest[:, 0], offsets, profile_index, scans.reshape(blocks, rows, tile_cols))
    exchange = functools.partial(
        lax.all_to_all, axis_name=("row", "col"), split_axis=0, concat_axis=0, tiled=True
    )
    got_meta = exchange(meta.reshape(device_count, capacity)).reshape(slots)
    got = exchange(payload.reshape(device_count, capacity * rows, tile_cols))
    got = got.reshape(slots, rows, tile_cols)
    weights = jnp.broadcast_to(
        profiles[:, :, None, :], (profile_count, strip_rows, channels, tile_cols)
    ).reshape(profile_count, rows, tile_cols)
    weights = jnp.concatenate([weights, jnp.zeros((1, rows, tile_cols), f32)], 0)
    embed = (
        embed_weight.reshape(channels, PATCH, PATCH, width)
        .transpose(2, 1, 0, 3)
        .reshape(PATCH, PATCH * channels, width)
    )
    bias = window_bias(token_cols)
    stream, inputs = pl.pallas_call(
        merge_kernel,
        out_shape=(
            jax.ShapeDtypeStruct((count, width), f32),
            jax.ShapeDtypeStruct((count, width), bf16),
        ),
        in_specs=[SMEM, VMEM, VMEM, VMEM, VMEM],
        out_specs=(VMEM, VMEM),
        scratch_shapes=[
            pltpu.VMEM((tile_rows * channels, tile_cols), f32),
            pltpu.VMEM((tile_rows * channels, tile_cols), f32),
            pltpu.VMEM((TOK_H * tile_cols, PATCH * channels), f32),
        ],
        compiler_params=params,
        name="merge",
    )(got_meta, got, weights, embed, attn_gain[:1])
    padded = (TOK_H + 2 * RADIUS) * token_cols
    beside = (TOK_H + 2 * RADIUS) * 2 * RADIUS
    for l in range(layers):
        last = l == layers - 1
        centre, side = surround(inputs, token_cols)
        if last:
            shapes = jax.ShapeDtypeStruct((count, width), bf16)
            specs = VMEM
        else:
            shapes = (
                jax.ShapeDtypeStruct((count, width), f32),
                jax.ShapeDtypeStruct((count, width), bf16),
            )
            specs = (VMEM, VMEM)
        result = pl.pallas_call(
            functools.partial(layer_kernel, last, token_cols),
            out_shape=shapes,
            grid=(1,),
            in_specs=[
                VMEM,
                VMEM,
                pl.BlockSpec((None, width, 3 * width), lambda i, l=l: (l, 0, 0)),
                pl.BlockSpec((None, width, width), lambda i, l=l: (l, 0, 0)),
                VMEM,
                VMEM,
                VMEM,
            ],
            out_specs=specs,
            scratch_shapes=[
                pltpu.VMEM((count, width), bf16),
                pltpu.VMEM((padded, 2 * width), bf16),
                pltpu.VMEM((beside, 2 * width), bf16),
            ],
            compiler_params=params,
            name="layer",
        )(centre, side, qkv_weight, out_weight, stream, bias, attn_gain[min(l + 1, layers - 1)][None])
        if last:
            return result.reshape(TOK_H, token_cols, width)
        stream, inputs = result


def solution(mesh):
    placed = (
        P(("row", "col"), None, None, None),
        P(("row", "col"), None),
        P(("row", "col")),
        P(("row", "col")),
        P(),
        P(),
        P(),
        P(),
        P(),
    )
    return jax.shard_map(
        per_device, mesh=mesh, in_specs=placed, out_specs=P("row", "col", None), check_vma=False
    )
```

time: 376 us -> 176 us (0.47); the launches traced: 369 us -> 173 us
  local copies, waits for them, and re-layouts: 145 us -> 8.65 us
  matrix products: 67 us -> 0 us
  Pallas kernels: 0 us -> 57.6 us
  waiting for transfers between devices: 93.8 us -> 59.4 us
  starting transfers between devices: 43.2 us -> 30.5 us
  other arithmetic: 18.8 us -> 7.07 us
  blocking collectives: 0 us -> 9.86 us
    pallas_call x0 -> x4, Pallas kernels: none -> 57.6 us  [the longest x2 43 us: per_device(): pl.pallas_call(functools.partial(layer_kernel, last, token_cols), out_sha...]
    dot_general x12 -> x0, matrix products: 50.6 us -> none  [the longest x2 14.7 us: per_device(): jnp.einsum('bhqk,bkhd->bqhd', attention, values, preferred_element_type=j...]
    all_to_all x3 -> x1, waiting for transfers between devices: 84.1 us -> 40.7 us  [per_device(): got = exchange(payload.reshape(device_count, capacity * rows, tile_cols))]
    another operation x20 -> x0, local copies, waits for them, and re-layouts: 37.9 us -> none  [the longest x18 32.6 us: per_device(): jnp.stack([keyvals[bi * sub_rows:bi * sub_rows + win_rows, bj * sub_cols:...]
    reshape x6 -> x3, local copies, waits for them, and re-layouts: 33 us -> 2.19 us  [the longest x1 1.55 us: per_device(): embed_weight.reshape(channels, PATCH, PATCH, width).transpose(2, 1, 0, 3)]
    sub x2 -> x0, matrix products: 16.4 us -> none  [per_device(): exponent = jnp.exp(logits - row_max)]
    transpose x5 -> x0, local copies, waits for them, and re-layouts: 16.1 us -> none  [the longest x1 10.6 us: per_device(): patches = merged.reshape(TOK_H, 8, channels, token_cols, 8).transpose(0,...]
    all_to_all x3 -> x1, starting transfers between devices: 18.6 us -> 5.88 us  [per_device(): got = exchange(payload.reshape(device_count, capacity * rows, tile_cols))]
  transfers between devices with their start and end apart: 11 -> 9, of which waited for: 6 -> 9; matrix products, arithmetic and copies ran while one was open for 14% -> 3% of each run, Pallas kernels for 0% -> 0%
where the time goes in v1:
time: 176 us; the launch traced here: 173 us
  waiting for transfers between devices  59.4 us (34%)
  Pallas kernels  57.6 us (33%)
  starting transfers between devices  30.5 us (17%)
  blocking collectives  9.86 us (6%)
  local copies, waits for them, and re-layouts  8.65 us (5%)
  other arithmetic  7.07 us (4%)
    pallas_call x2, Pallas kernels, per_device(): pl.pallas_call(functools.partial(layer_kernel, last, token_cols), out_sha...  43 us
    all_to_all x1, waiting for transfers between devices, per_device(): got = exchange(payload.reshape(device_count, capacity * rows, tile_cols))  40.7 us
    ppermute x8, starting transfers between devices, shifted(): return lax.ppermute(cells, axis, pairs)  24.6 us
    ppermute x8, waiting for transfers between devices, shifted(): return lax.ppermute(cells, axis, pairs)  18.8 us
    pallas_call x1, Pallas kernels, per_device(): pl.pallas_call(merge_kernel, out_shape=(jax.ShapeDtypeStruct((count, widt...  10.2 us
    all_to_all x1, blocking collectives, per_device(): got_meta = exchange(meta.reshape(device_count, capacity)).reshape(slots)  9.86 us
    all_to_all x1, starting transfers between devices, per_device(): got = exchange(payload.reshape(device_count, capacity * rows, tile_cols))  5.88 us
    pallas_call x1, Pallas kernels, per_device(): pl.pallas_call(functools.partial(place_kernel, capacity, profile_count *...  4.32 us
  transfers between devices with their start and end apart: 9, of which 9 were waited for; matrix products, arithmetic and copies ran while one was open for 3% of the time, Pallas kernels for 0%

profile of v1, /device:TPU:20, one launch (start us, length us, event | category | flops | bytes accessed | tf_op | source)
XLA Modules:
  0.0 173.4 jit_solution(6041124623384844196)
XLA Ops:
  0.0 0.0 copy-start
  0.0 4.3 %place.1 = (bf16[256,32,128]{2,1,0:T(8,128)(2,1)}, s32[256]{0:T(256)}) custom-call(s32[128]{0:T(128)} %bitcast.40, s32[128]{0:T(128)} %offsets.1, s32[128]{0:T(128)} %profile.1, f32[128,32,128]{2,1,0:T(8,128)} %bitcast.30), custom_call_target="tpu_custom_call" | custom-call | tf_op jit(solution)/shard_map/place/pallas_call | solution.py:255
  4.3 0.8 all_to_all.9
  5.1 9.9 %all_to_all.14 = s32[32,1,8]{2,1,0:T(1,128)S(1)} all-to-all(s32[32,1,8]{2,1,0:T(1,128)S(1)} %bitcast.39), channel_id=1, replica_groups=mesh['row'=4,'col'=8] {'row','col'}, dimensions={0} | all-to-all | bytes 2048 | tf_op jit(solution)/shard_map/all_to_all | solution.py:270
  15.0 5.9 %all-to-all-start.1 = ((bf16[32,256,128]{2,1,0:T(8,128)(2,1)}), bf16[32,256,128]{2,1,0:T(8,128)(2,1)S(1)}, u32[]{:S(2)}, u32[]{:S(2)}) async-start(bf16[32,256,128]{2,1,0:T(8,128)(2,1)} %bitcast.31), calls=%async_computation.1 | async-start | bytes 4194304 | tf_op jit(solution)/shard_map/all_to_all | solution.py:271
  20.8 0.0 copy-done.4
  20.9 0.0 copy-start.5
  20.9 1.5 copy.15
  22.4 0.0 copy-done
  22.4 0.7 concatenate.32.weights
  23.2 0.0 copy-done.5
  23.2 0.6 fusion.10
  23.8 0.2 fusion
  24.0 0.5 broadcast.258
  24.5 0.7 reduce.3
  25.2 0.6 reshape.230.meta
  25.8 40.7 %all-to-all-done.1 = bf16[32,256,128]{2,1,0:T(8,128)(2,1)S(1)} async-done(((bf16[32,256,128]{2,1,0:T(8,128)(2,1)}), bf16[32,256,128]{2,1,0:T(8,128)(2,1)S(1)}, u32[]{:S(2)}, u32[]{:S(2)}) %all-to-all-start.1) | async-done | bytes 2097184 | tf_op jit(solution)/shard_map/all_to_all | solution.py:271
  66.5 1.3 copy-done.1
  67.8 10.2 %merge.1 = (f32[512,1024]{1,0:T(8,128)}, bf16[512,1024]{1,0:T(8,128)(2,1)}) custom-call(s32[256]{0:T(256)} %reshape.230.meta, bf16[256,32,128]{2,1,0:T(8,128)(2,1)} %bitcast.26, f32[17,32,128]{2,1,0:T(8,128)} %concatenate.32.weights, bf16[8,64,1024]{2,1,0:T(8,128)(2,1)} %bitcast.29, f32[1,1024]{1,0:T(1,128)} %get-tuple-element.26.gain), custom_call_target="tpu_custom_call" | custom-call | tf_op jit(solution)/shard_map/merge/pallas_call | solution.py:283
  78.1 1.0 fusion.9
  79.0 3.3 %collective-permute-start.1 = (bf16[4,16,1024]{2,1,0:T(8,128)(2,1)S(1)}, bf16[4,16,1024]{2,1,0:T(8,128)(2,1)S(1)}, u32[]{:S(2)}, u32[]{:S(2)}) collective-permute-start(bf16[4,16,1024]{2,1,0:T(8,128)(2,1)S(1)} %bitcast.36), channel_id=1, source_target_pairs={{8,0},{16,8},{24,16},{9,1},{17,9},{25,17},{10,2},{18,10},{26,18},{... | collective-permute-start | bytes 393224 | tf_op jit(solution)/shard_map/ppermute | solution.py:184
  82.4 2.5 %collective-permute-start = (bf16[4,16,1024]{2,1,0:T(8,128)(2,1)S(1)}, bf16[4,16,1024]{2,1,0:T(8,128)(2,1)S(1)}, u32[]{:S(2)}, u32[]{:S(2)}) collective-permute-start(bf16[4,16,1024]{2,1,0:T(8,128)(2,1)S(1)} %bitcast.35), channel_id=1, source_target_pairs={{0,8},{8,16},{16,24},{1,9},{9,17},{17,25},{2,10},{10,18},{18,26},{... | collective-permute-start | bytes 393224 | tf_op jit(solution)/shard_map/ppermute | solution.py:184
  84.9 1.4 collective-permute-done.1
  86.3 3.3 %collective-permute-done = bf16[4,16,1024]{2,1,0:T(8,128)(2,1)S(1)} collective-permute-done((bf16[4,16,1024]{2,1,0:T(8,128)(2,1)S(1)}, bf16[4,16,1024]{2,1,0:T(8,128)(2,1)S(1)}, u32[]{:S(2)}, u32[]{:S(2)}) %collective-permute-start) | collective-permute-done | bytes 131104 | tf_op jit(solution)/shard_map/ppermute | solution.py:184
  89.6 1.4 pad_maximum_fusion
  91.0 0.0 copy-start.2
  91.0 0.3 fusion.7
  91.3 1.9 %collective-permute-start.2 = (bf16[40,4,1024]{2,1,0:T(4,128)(2,1)S(1)}, bf16[40,4,1024]{2,1,0:T(4,128)(2,1)S(1)}, u32[]{:S(2)}, u32[]{:S(2)}) collective-permute-start(bf16[40,4,1024]{2,1,0:T(4,128)(2,1)S(1)} %get-tuple-element.19), channel_id=1, source_target_pairs={{0,1},{1,2},{2,3},{3,4},{4,5},{5,6},{6,7},{8,9},{9,10},{10,11},{11... | collective-permute-start | bytes 983048 | tf_op jit(solution)/shard_map/ppermute | solution.py:184
  93.2 4.5 %collective-permute-start.3 = (bf16[40,4,1024]{2,1,0:T(4,128)(2,1)S(1)}, bf16[40,4,1024]{2,1,0:T(4,128)(2,1)S(1)}, u32[]{:S(2)}, u32[]{:S(2)}) collective-permute-start(bf16[40,4,1024]{2,1,0:T(4,128)(2,1)S(1)} %get-tuple-element.20), channel_id=1, source_target_pairs={{1,0},{2,1},{3,2},{4,3},{5,4},{6,5},{7,6},{9,8},{10,9},{11,10},{12... | collective-permute-start | bytes 983048 | tf_op jit(solution)/shard_map/ppermute | solution.py:184
  97.8 0.1 fusion.3
  97.9 1.0 and_select_fusion.bias
  98.8 1.8 %collective-permute-done.2 = bf16[40,4,1024]{2,1,0:T(4,128)(2,1)S(1)} collective-permute-done((bf16[40,4,1024]{2,1,0:T(4,128)(2,1)S(1)}, bf16[40,4,1024]{2,1,0:T(4,128)(2,1)S(1)}, u32[]{:S(2)}, u32[]{:S(2)}) %collective-permute-start.2) | collective-permute-done | bytes 327712 | tf_op jit(solution)/shard_map/ppermute | solution.py:184
  100.6 1.7 %collective-permute-done.3 = bf16[40,4,1024]{2,1,0:T(4,128)(2,1)S(1)} collective-permute-done((bf16[40,4,1024]{2,1,0:T(4,128)(2,1)S(1)}, bf16[40,4,1024]{2,1,0:T(4,128)(2,1)S(1)}, u32[]{:S(2)}, u32[]{:S(2)}) %collective-permute-start.3) | collective-permute-done | bytes 327712 | tf_op jit(solution)/shard_map/ppermute | solution.py:184
  102.3 1.2 maximum_bitcast_fusion.side
  103.5 22.2 %layer.2 = (f32[512,1024]{1,0:T(8,128)}, bf16[512,1024]{1,0:T(8,128)(2,1)}) custom-call(bf16[640,1024]{1,0:T(8,128)(2,1)} %bitcast.27, bf16[320,1024]{1,0:T(8,128)(2,1)} %maximum_bitcast_fusion.side, bf16[2,1024,3072]{2,1,0:T(8,128)(2,1)} %qkv.3, bf16[2,1024,1024]{2,1,0:T(8,128)(2,1)} %out_w.3, f32[512,1024]{1,0:T(8,128)} %get-tuple-element.14.stream, ...), custom_call_target="tpu_custom_call" | custom-call | tf_op jit(solution)/shard_map/layer/pallas_call | solution.py:313
  125.7 1.0 fusion.8
  126.7 3.9 %collective-permute-start.5 = (bf16[4,16,1024]{2,1,0:T(8,128)(2,1)S(1)}, bf16[4,16,1024]{2,1,0:T(8,128)(2,1)S(1)}, u32[]{:S(2)}, u32[]{:S(2)}) collective-permute-start(bf16[4,16,1024]{2,1,0:T(8,128)(2,1)S(1)} %bitcast.38), channel_id=1, source_target_pairs={{8,0},{16,8},{24,16},{9,1},{17,9},{25,17},{10,2},{18,10},{26,18},{... | collective-permute-start | bytes 393224 | tf_op jit(solution)/shard_map/ppermute | solution.py:184
  130.6 1.9 %collective-permute-start.4 = (bf16[4,16,1024]{2,1,0:T(8,128)(2,1)S(1)}, bf16[4,16,1024]{2,1,0:T(8,128)(2,1)S(1)}, u32[]{:S(2)}, u32[]{:S(2)}) collective-permute-start(bf16[4,16,1024]{2,1,0:T(8,128)(2,1)S(1)} %bitcast.37), channel_id=1, source_target_pairs={{0,8},{8,16},{16,24},{1,9},{9,17},{17,25},{2,10},{10,18},{18,26},{... | collective-permute-start | bytes 393224 | tf_op jit(solution)/shard_map/ppermute | solution.py:184
  132.5 2.4 %collective-permute-done.5 = bf16[4,16,1024]{2,1,0:T(8,128)(2,1)S(1)} collective-permute-done((bf16[4,16,1024]{2,1,0:T(8,128)(2,1)S(1)}, bf16[4,16,1024]{2,1,0:T(8,128)(2,1)S(1)}, u32[]{:S(2)}, u32[]{:S(2)}) %collective-permute-start.5) | collective-permute-done | bytes 131104 | tf_op jit(solution)/shard_map/ppermute | solution.py:184
  134.9 3.7 %collective-permute-done.4 = bf16[4,16,1024]{2,1,0:T(8,128)(2,1)S(1)} collective-permute-done((bf16[4,16,1024]{2,1,0:T(8,128)(2,1)S(1)}, bf16[4,16,1024]{2,1,0:T(8,128)(2,1)S(1)}, u32[]{:S(2)}, u32[]{:S(2)}) %collective-permute-start.4) | collective-permute-done | bytes 131104 | tf_op jit(solution)/shard_map/ppermute | solution.py:184
  138.6 1.4 pad_maximum_fusion.1
  140.0 0.3 fusion.6
  140.2 1.9 %collective-permute-start.6 = (bf16[40,4,1024]{2,1,0:T(4,128)(2,1)S(1)}, bf16[40,4,1024]{2,1,0:T(4,128)(2,1)S(1)}, u32[]{:S(2)}, u32[]{:S(2)}) collective-permute-start(bf16[40,4,1024]{2,1,0:T(4,128)(2,1)S(1)} %get-tuple-element.17), channel_id=1, source_target_pairs={{0,1},{1,2},{2,3},{3,4},{4,5},{5,6},{6,7},{8,9},{9,10},{10,11},{11... | collective-permute-start | bytes 983048 | tf_op jit(solution)/shard_map/ppermute | solution.py:184
  142.2 4.5 %collective-permute-start.7 = (bf16[40,4,1024]{2,1,0:T(4,128)(2,1)S(1)}, bf16[40,4,1024]{2,1,0:T(4,128)(2,1)S(1)}, u32[]{:S(2)}, u32[]{:S(2)}) collective-permute-start(bf16[40,4,1024]{2,1,0:T(4,128)(2,1)S(1)} %get-tuple-element.18), channel_id=1, source_target_pairs={{1,0},{2,1},{3,2},{4,3},{5,4},{6,5},{7,6},{9,8},{10,9},{11,10},{12... | collective-permute-start | bytes 983048 | tf_op jit(solution)/shard_map/ppermute | solution.py:184
  146.7 4.1 %collective-permute-done.6 = bf16[40,4,1024]{2,1,0:T(4,128)(2,1)S(1)} collective-permute-done((bf16[40,4,1024]{2,1,0:T(4,128)(2,1)S(1)}, bf16[40,4,1024]{2,1,0:T(4,128)(2,1)S(1)}, u32[]{:S(2)}, u32[]{:S(2)}) %collective-permute-start.6) | collective-permute-done | bytes 327712 | tf_op jit(solution)/shard_map/ppermute | solution.py:184
  150.8 0.5 collective-permute-done.7
  151.3 1.2 maximum_bitcast_fusion.1.side
  152.5 20.9 %layer.3 = bf16[512,1024]{1,0:T(8,128)(2,1)} custom-call(bf16[640,1024]{1,0:T(8,128)(2,1)} %bitcast.28, bf16[320,1024]{1,0:T(8,128)(2,1)} %maximum_bitcast_fusion.1.side, bf16[2,1024,3072]{2,1,0:T(8,128)(2,1)} %qkv.3, bf16[2,1024,1024]{2,1,0:T(8,128)(2,1)} %out_w.3, f32[512,1024]{1,0:T(8,128)} %get-tuple-element.16.stream, ...), custom_call_target="tpu_custom_call" | custom-call | tf_op jit(solution)/shard_map/layer/pallas_call | solution.py:313
  (14 shorter events, 0.1 us)
Async XLA Ops:
  0.0 22.4 %copy-start = (f32[16,4,128]{2,1,0:T(4,128)S(1)}, f32[16,4,128]{2,1,0:T(4,128)}, u32[]{:S(2)}) copy-start(f32[16,4,128]{2,1,0:T(4,128)} %param.13) | copy-start | bytes 98308
  15.0 5.9 %copy-start.4 = (bf16[512,1024]{1,0:T(8,128)(2,1)S(1)}, bf16[512,1024]{1,0:T(8,128)(2,1)}, u32[]{:S(2)}) copy-start(bf16[512,1024]{1,0:T(8,128)(2,1)} %param.14) | copy-start | bytes 3145732
  15.0 51.5 %all-to-all-start.1 = ((bf16[32,256,128]{2,1,0:T(8,128)(2,1)}), bf16[32,256,128]{2,1,0:T(8,128)(2,1)S(1)}, u32[]{:S(2)}, u32[]{:S(2)}) async-start(bf16[32,256,128]{2,1,0:T(8,128)(2,1)} %bitcast.31), calls=%async_computation.1 | async-start | bytes 4194304 | tf_op jit(solution)/shard_map/all_to_all | solution.py:271
  20.9 2.4 %copy-start.5 = (f32[2,1024]{1,0:T(2,128)S(1)}, f32[2,1024]{1,0:T(2,128)}, u32[]{:S(2)}) copy-start(f32[2,1024]{1,0:T(2,128)} %param.15) | copy-start | bytes 24580
  66.5 1.3 copy-start.1
  79.0 7.3 %collective-permute-start.1 = (bf16[4,16,1024]{2,1,0:T(8,128)(2,1)S(1)}, bf16[4,16,1024]{2,1,0:T(8,128)(2,1)S(1)}, u32[]{:S(2)}, u32[]{:S(2)}) collective-permute-start(bf16[4,16,1024]{2,1,0:T(8,128)(2,1)S(1)} %bitcast.36), channel_id=1, source_target_pairs={{8,0},{16,8},{24,16},{9,1},{17,9},{25,17},{10,2},{18,10},{26,18},{... | collective-permute-start | bytes 393224 | tf_op jit(solution)/shard_map/ppermute | solution.py:184
  82.4 7.3 %collective-permute-start = (bf16[4,16,1024]{2,1,0:T(8,128)(2,1)S(1)}, bf16[4,16,1024]{2,1,0:T(8,128)(2,1)S(1)}, u32[]{:S(2)}, u32[]{:S(2)}) collective-permute-start(bf16[4,16,1024]{2,1,0:T(8,128)(2,1)S(1)} %bitcast.35), channel_id=1, source_target_pairs={{0,8},{8,16},{16,24},{1,9},{9,17},{17,25},{2,10},{10,18},{18,26},{... | collective-permute-start | bytes 393224 | tf_op jit(solution)/shard_map/ppermute | solution.py:184
  91.0 12.5 %copy-start.2 = (bf16[40,16,1024]{2,1,0:T(8,128)(2,1)}, bf16[40,16,1024]{2,1,0:T(8,128)(2,1)S(1)}, u32[]{:S(2)}) copy-start(bf16[40,16,1024]{2,1,0:T(8,128)(2,1)S(1)} %pad_maximum_fusion) | copy-start | bytes 3932164
  91.3 9.3 %collective-permute-start.2 = (bf16[40,4,1024]{2,1,0:T(4,128)(2,1)S(1)}, bf16[40,4,1024]{2,1,0:T(4,128)(2,1)S(1)}, u32[]{:S(2)}, u32[]{:S(2)}) collective-permute-start(bf16[40,4,1024]{2,1,0:T(4,128)(2,1)S(1)} %get-tuple-element.19), channel_id=1, source_target_pairs={{0,1},{1,2},{2,3},{3,4},{4,5},{5,6},{6,7},{8,9},{9,10},{10,11},{11... | collective-permute-start | bytes 983048 | tf_op jit(solution)/shard_map/ppermute | solution.py:184
  93.2 9.1 %collective-permute-start.3 = (bf16[40,4,1024]{2,1,0:T(4,128)(2,1)S(1)}, bf16[40,4,1024]{2,1,0:T(4,128)(2,1)S(1)}, u32[]{:S(2)}, u32[]{:S(2)}) collective-permute-start(bf16[40,4,1024]{2,1,0:T(4,128)(2,1)S(1)} %get-tuple-element.20), channel_id=1, source_target_pairs={{1,0},{2,1},{3,2},{4,3},{5,4},{6,5},{7,6},{9,8},{10,9},{11,10},{12... | collective-permute-start | bytes 983048 | tf_op jit(solution)/shard_map/ppermute | solution.py:184
  126.7 8.2 %collective-permute-start.5 = (bf16[4,16,1024]{2,1,0:T(8,128)(2,1)S(1)}, bf16[4,16,1024]{2,1,0:T(8,128)(2,1)S(1)}, u32[]{:S(2)}, u32[]{:S(2)}) collective-permute-start(bf16[4,16,1024]{2,1,0:T(8,128)(2,1)S(1)} %bitcast.38), channel_id=1, source_target_pairs={{8,0},{16,8},{24,16},{9,1},{17,9},{25,17},{10,2},{18,10},{26,18},{... | collective-permute-start | bytes 393224 | tf_op jit(solution)/shard_map/ppermute | solution.py:184
  130.6 8.0 %collective-permute-start.4 = (bf16[4,16,1024]{2,1,0:T(8,128)(2,1)S(1)}, bf16[4,16,1024]{2,1,0:T(8,128)(2,1)S(1)}, u32[]{:S(2)}, u32[]{:S(2)}) collective-permute-start(bf16[4,16,1024]{2,1,0:T(8,128)(2,1)S(1)} %bitcast.37), channel_id=1, source_target_pairs={{0,8},{8,16},{16,24},{1,9},{9,17},{17,25},{2,10},{10,18},{18,26},{... | collective-permute-start | bytes 393224 | tf_op jit(solution)/shard_map/ppermute | solution.py:184
  140.0 12.5 %copy-start.3 = (bf16[40,16,1024]{2,1,0:T(8,128)(2,1)}, bf16[40,16,1024]{2,1,0:T(8,128)(2,1)S(1)}, u32[]{:S(2)}) copy-start(bf16[40,16,1024]{2,1,0:T(8,128)(2,1)S(1)} %pad_maximum_fusion.1) | copy-start | bytes 3932164
  140.2 10.5 %collective-permute-start.6 = (bf16[40,4,1024]{2,1,0:T(4,128)(2,1)S(1)}, bf16[40,4,1024]{2,1,0:T(4,128)(2,1)S(1)}, u32[]{:S(2)}, u32[]{:S(2)}) collective-permute-start(bf16[40,4,1024]{2,1,0:T(4,128)(2,1)S(1)} %get-tuple-element.17), channel_id=1, source_target_pairs={{0,1},{1,2},{2,3},{3,4},{4,5},{5,6},{6,7},{8,9},{9,10},{10,11},{11... | collective-permute-start | bytes 983048 | tf_op jit(solution)/shard_map/ppermute | solution.py:184
  142.2 9.1 %collective-permute-start.7 = (bf16[40,4,1024]{2,1,0:T(4,128)(2,1)S(1)}, bf16[40,4,1024]{2,1,0:T(4,128)(2,1)S(1)}, u32[]{:S(2)}, u32[]{:S(2)}) collective-permute-start(bf16[40,4,1024]{2,1,0:T(4,128)(2,1)S(1)} %get-tuple-element.18), channel_id=1, source_target_pairs={{1,0},{2,1},{3,2},{4,3},{5,4},{6,5},{7,6},{9,8},{10,9},{11,10},{12... | collective-permute-start | bytes 983048 | tf_op jit(solution)/shard_map/ppermute | solution.py:184

commit v2 on v1

v2 whole, which is shorter than its diff:
```python
import functools

import jax
import jax.numpy as jnp
from jax import lax
from jax.experimental import pallas as pl
from jax.experimental.pallas import tpu as pltpu
from jax.sharding import PartitionSpec as P

HEADS = 16
RADIUS = 4
TOK_H = 32
PATCH = 8
BAND = 8

VMEM = pl.BlockSpec(memory_space=pltpu.VMEM)
SMEM = pl.BlockSpec(memory_space=pltpu.SMEM)


def place_kernel(capacity, dest, offsets, profile, scans, payload, index, count):
    blocks, rows, lanes = scans.shape
    tiles = payload.shape[0]
    payload[...] = jnp.zeros_like(payload)
    index[...] = jnp.zeros_like(index)
    first = lax.broadcasted_iota(jnp.int32, (1, lanes), 1) < lanes // 2

    def clear(i, c):
        count[i] = 0
        return c

    lax.fori_loop(0, tiles, clear, 0, unroll=8)

    def put(b, c):
        tile = dest[b]
        rank = count[tile]
        count[tile] = rank + 1
        payload[tile, pl.ds(pl.multiple_of(rank * rows, rows), rows), :] = scans[b].astype(
            jnp.bfloat16
        )
        named = jnp.where(first, offsets[b], profile[b] + 1).astype(jnp.float32)
        index[tile, pl.ds(rank, 1), :] = named
        return c

    lax.fori_loop(0, blocks, put, 0, unroll=4)
    payload[:, capacity * rows :, :] = index[...].astype(jnp.bfloat16)


def normed(stream, gain_row):
    centre = jnp.mean(stream, -1, keepdims=True)
    spread = jnp.mean(jnp.square(stream - centre), -1, keepdims=True)
    return ((stream - centre) * lax.rsqrt(spread + 1e-05) * gain_row).astype(jnp.bfloat16)


def edges(cells, token_cols):
    tokens = cells.shape[0]
    each = tokens // token_cols * RADIUS
    slot = lax.broadcasted_iota(jnp.int32, (2 * each, tokens), 0)
    token = lax.broadcasted_iota(jnp.int32, (2 * each, tokens), 1)
    right = slot >= each
    slot = jnp.where(right, slot - each, slot)
    col = slot % RADIUS + jnp.where(right, token_cols - RADIUS, 0)
    chosen = (token == slot // RADIUS * token_cols + col).astype(jnp.float32)
    picked = jnp.dot(
        chosen.astype(jnp.bfloat16), cells, preferred_element_type=jnp.float32
    ).astype(jnp.bfloat16)
    return picked[:each], picked[each:]


def merge_kernel(
    rows, token_cols, meta, got, weights, embed, gain, stream, inputs, left, right, num, den, turned
):
    tiles, _, lanes = got.shape
    capacity = meta.shape[0] // tiles
    num[...] = jnp.zeros_like(num)
    den[...] = jnp.ones_like(den)

    def add_tile(t, c):
        for r in range(capacity):
            m = meta[t * capacity + r]
            w = weights[m >> 8]
            at = pl.ds(pl.multiple_of((m & 255) * 8, 8), rows)
            num[at, :] += got[t, r * rows : (r + 1) * rows, :].astype(jnp.float32) * w
            den[at, :] += w
        return c

    lax.fori_loop(0, tiles, add_tile, 0)
    group = PATCH * 8

    def turn(i, c):
        at = pl.ds(pl.multiple_of(i * group, group), group)
        merged = (num[at, :] / den[at, :]).astype(jnp.bfloat16).astype(jnp.float32)
        turned[pl.ds(pl.multiple_of(i * lanes, lanes), lanes), :] = merged.T
        return c

    lax.fori_loop(0, TOK_H, turn, 0, unroll=4)
    part = BAND * token_cols

    def embed_part(k, c):
        total = None
        for q in range(PATCH):
            lhs = turned[pl.ds(k * part * PATCH + q, part, stride=PATCH), :]
            term = jnp.dot(
                lhs.astype(jnp.bfloat16), embed[q], preferred_element_type=jnp.float32
            )
            total = term if total is None else total + term
        at = pl.ds(pl.multiple_of(k * part, part), part)
        stream[at, :] = total
        cells = normed(total, gain[...])
        inputs[at, :] = cells
        edge = pl.ds(pl.multiple_of(k * BAND * RADIUS, BAND * RADIUS), BAND * RADIUS)
        left[edge, :], right[edge, :] = edges(cells, token_cols)
        return c

    lax.fori_loop(0, TOK_H // BAND, embed_part, 0)


def layer_kernel(layer, last, token_cols, sizes, x, own_left, own_right, qkv, out_w, stream, bias, gain, *refs):
    outs, refs = (refs[:1], refs[1:]) if last else (refs[:4], refs[4:])
    q_ref, kc, kl, kr, w, wo, x_rows, x_left, x_right, w_sem, send, recv = refs
    width = wo.shape[0]
    head_dim = width // HEADS
    count = x.shape[0]
    halo = RADIUS * token_cols
    corner = RADIUS * RADIUS
    side = TOK_H * RADIUS
    loads = [
        pltpu.make_async_copy(
            qkv.at[layer, :, n * width : (n + 1) * width], w.at[n], w_sem.at[n]
        )
        for n in range(3)
    ] + [pltpu.make_async_copy(out_w.at[layer], wo, w_sem.at[3])]
    for load in loads:
        load.start()

    row, col = lax.axis_index("row"), lax.axis_index("col")
    up, down = row > 0, row < sizes[0] - 1
    west, east = col > 0, col < sizes[1] - 1
    moves = [
        (-1, 0, up, x.at[:halo], x_rows.at[halo:], x_rows.at[:halo]),
        (1, 0, down, x.at[count - halo :], x_rows.at[:halo], x_rows.at[halo:]),
        (0, -1, west, own_left, x_right.at[corner : corner + side], x_left.at[corner : corner + side]),
        (0, 1, east, own_right, x_left.at[corner : corner + side], x_right.at[corner : corner + side]),
        (-1, -1, up & west, own_left.at[:corner], x_right.at[corner + side :], x_left.at[:corner]),
        (-1, 1, up & east, own_right.at[:corner], x_left.at[corner + side :], x_right.at[:corner]),
        (1, -1, down & west, own_left.at[side - corner :], x_right.at[:corner], x_left.at[corner + side :]),
        (1, 1, down & east, own_right.at[side - corner :], x_left.at[:corner], x_right.at[corner + side :]),
    ]
    opposite = [1, 0, 3, 2, 7, 6, 5, 4]
    barrier = pltpu.get_barrier_semaphore()
    mesh_ids = pl.DeviceIdType.MESH
    for dr, dc, there, _, _, _ in moves:

        @pl.when(there)
        def _(dr=dr, dc=dc):
            pl.semaphore_signal(
                barrier, inc=1, device_id=(row + dr, col + dc), device_id_type=mesh_ids
            )

    for _, _, there, _, _, here in moves:

        @pl.when(jnp.logical_not(there))
        def _(here=here):
            here[...] = jnp.zeros(here.shape, here.dtype)

    rows_near = 1 + up.astype(jnp.int32) + down.astype(jnp.int32)
    cols_near = 1 + west.astype(jnp.int32) + east.astype(jnp.int32)
    pl.semaphore_wait(barrier, rows_near * cols_near - 1)
    copies = []
    for n, (dr, dc, there, source, lands, _) in enumerate(moves):
        copies.append(
            pltpu.make_async_remote_copy(
                src_ref=source,
                dst_ref=lands,
                send_sem=send.at[n],
                recv_sem=recv.at[n],
                device_id=(row + dr, col + dc),
                device_id_type=mesh_ids,
            )
        )

        @pl.when(there)
        def _(copy=copies[-1]):
            copy.start()

    def times(rows, weight, target, at, base, scale=None):
        step = 512

        def part(n, c):
            cols = pl.ds(pl.multiple_of(n * step, step), step)
            to = pl.ds(pl.multiple_of(base + n * step, step), step)
            y = jnp.dot(
                rows[...], weight[:, cols], preferred_element_type=jnp.float32
            ).astype(jnp.bfloat16)
            target[at, to] = y if scale is None else (y * scale).astype(jnp.bfloat16)
            return c

        lax.fori_loop(0, width // step, part, 0)

    middle = slice(halo, halo + count)
    loads[0].wait()
    times(x, w.at[0], q_ref, slice(0, count), 0, head_dim ** (-0.5))
    for n in (1, 2):
        loads[n].wait()
        times(x, w.at[n], kc, middle, (n - 1) * width)
    for n, (_, _, there, _, _, here) in enumerate(moves):

        @pl.when(there)
        def _(n=n, here=here):
            copies[n].wait_send()
            pltpu.make_async_remote_copy(
                src_ref=here,
                dst_ref=here,
                send_sem=send.at[n],
                recv_sem=recv.at[opposite[n]],
                device_id=(row + moves[n][0], col + moves[n][1]),
                device_id_type=mesh_ids,
            ).wait_recv()

    for n in (1, 2):
        base = (n - 1) * width
        times(x_rows.at[:halo], w.at[n], kc, slice(0, halo), base)
        times(x_rows.at[halo:], w.at[n], kc, slice(halo + count, 2 * halo + count), base)
        times(x_left, w.at[n], kl, slice(0, side + 2 * corner), base)
        times(x_right, w.at[n], kr, slice(0, side + 2 * corner), base)
    loads[3].wait()
    queries = BAND * token_cols
    c_keys = (BAND + 2 * RADIUS) * token_cols
    s_keys = (BAND + 2 * RADIUS) * RADIUS
    pair = 2 * head_dim
    low = lax.broadcasted_iota(jnp.int32, (queries, pair), 1) < head_dim

    def band(b, carry):
        q_at = pl.ds(pl.multiple_of(b * queries, queries), queries)
        c_at = pl.ds(pl.multiple_of(b * queries, queries), c_keys)
        s_at = pl.ds(pl.multiple_of(b * BAND * RADIUS, BAND * RADIUS), s_keys)
        band_bias = bias[b]
        both = jnp.concatenate([band_bias, band_bias], 0)
        ones = jnp.ones((c_keys + 2 * s_keys, pair), jnp.bfloat16)
        pieces = []
        for h in range(HEADS // 2):
            cols = slice(h * pair, (h + 1) * pair)
            v_cols = slice(width + h * pair, width + (h + 1) * pair)
            q = q_ref[q_at, cols]
            zero = jnp.zeros_like(q)
            q2 = jnp.concatenate([jnp.where(low, q, zero), jnp.where(low, zero, q)], 0)
            k = jnp.concatenate([kc[c_at, cols], kl[s_at, cols], kr[s_at, cols]], 0)
            v = jnp.concatenate([kc[c_at, v_cols], kl[s_at, v_cols], kr[s_at, v_cols]], 0)
            logits = lax.dot_general(
                q2, k, (((1,), (1,)), ((), ())), preferred_element_type=jnp.float32
            )
            logits = logits + both
            top_logit = jnp.max(logits, -1, keepdims=True)
            weight = jnp.exp(logits - top_logit).astype(jnp.bfloat16)
            summed = jnp.dot(
                weight, jnp.concatenate([v, ones], 1), preferred_element_type=jnp.float32
            )
            share = summed[:, :pair] / summed[:, pair:]
            pieces.append(jnp.where(low, share[:queries], share[queries:]).astype(jnp.bfloat16))
        attended = jnp.concatenate(pieces, 1)
        total = stream[q_at, :] + jnp.dot(attended, wo[...], preferred_element_type=jnp.float32)
        if last:
            outs[0][q_at, :] = total.astype(jnp.bfloat16)
        else:
            outs[0][q_at, :] = total
            cells = normed(total, gain[...])
            outs[1][q_at, :] = cells
            edge = pl.ds(pl.multiple_of(b * BAND * RADIUS, BAND * RADIUS), BAND * RADIUS)
            outs[2][edge, :], outs[3][edge, :] = edges(cells, token_cols)
        return carry

    lax.fori_loop(0, count // queries, band, 0)


def window_bias(token_cols):
    bands = TOK_H // BAND
    win = BAND + 2 * RADIUS
    q = jnp.arange(BAND * token_cols, dtype=jnp.int32)
    q_row, q_col = q // token_cols, q % token_cols
    c = jnp.arange(win * token_cols, dtype=jnp.int32)
    s = jnp.arange(win * RADIUS, dtype=jnp.int32)
    k_row = jnp.concatenate([c // token_cols, s // RADIUS, s // RADIUS]) - RADIUS
    k_col = jnp.concatenate([c % token_cols, s % RADIUS - RADIUS, s % RADIUS + token_cols])
    near = (jnp.abs(k_row[None] - q_row[:, None]) <= RADIUS) & (
        jnp.abs(k_col[None] - q_col[:, None]) <= RADIUS
    )
    g_row = (
        lax.axis_index("row") * TOK_H
        + jnp.arange(bands, dtype=jnp.int32)[:, None] * BAND
        + k_row[None]
    )
    g_col = lax.axis_index("col") * token_cols + k_col
    inside = (
        (g_row >= 0)
        & (g_row < TOK_H * lax.axis_size("row"))
        & (g_col >= 0)[None]
        & (g_col < token_cols * lax.axis_size("col"))[None]
    )
    return jnp.where(near[None] & inside[:, None, :], 0.0, -1e30).astype(jnp.float32)


def per_device(
    scans, dest, offsets, profile_index, profiles, embed_weight, attn_gain, qkv_weight, out_weight
):
    device_count = lax.axis_size("row") * lax.axis_size("col")
    blocks, strip_rows, channels, tile_cols = scans.shape
    token_cols = tile_cols // PATCH
    count = TOK_H * token_cols
    tile_rows = TOK_H * PATCH
    profile_count = profiles.shape[0]
    width = embed_weight.shape[1]
    layers = qkv_weight.shape[0]
    capacity = max(2, 2 * blocks // device_count)
    slots = device_count * capacity
    rows = strip_rows * channels
    extra = -(-capacity // 16) * 16
    f32, bf16 = jnp.float32, jnp.bfloat16
    params = pltpu.CompilerParams(vmem_limit_bytes=56 * 2**20)

    payload = pl.pallas_call(
        functools.partial(place_kernel, capacity),
        out_shape=jax.ShapeDtypeStruct((device_count, capacity * rows + extra, tile_cols), bf16),
        in_specs=[SMEM, SMEM, SMEM, VMEM],
        out_specs=VMEM,
        scratch_shapes=[
            pltpu.VMEM((device_count, extra, tile_cols), f32),
            pltpu.SMEM((device_count,), jnp.int32),
        ],
        compiler_params=params,
        name="place",
    )(dest[:, 0], offsets, profile_index, scans.reshape(blocks, rows, tile_cols))
    got = lax.all_to_all(payload, ("row", "col"), split_axis=0, concat_axis=0, tiled=True)
    named = got[:, capacity * rows : capacity * rows + capacity, :]
    meta = (named[:, :, 0] + named[:, :, tile_cols // 2].astype(f32) * 256.0).astype(jnp.int32)
    meta = meta.reshape(slots)
    weights = jnp.broadcast_to(
        profiles[:, :, None, :], (profile_count, strip_rows, channels, tile_cols)
    ).reshape(profile_count, rows, tile_cols)
    weights = jnp.concatenate([jnp.zeros((1, rows, tile_cols), f32), weights], 0)
    embed = (
        embed_weight.reshape(channels, PATCH, PATCH, width)
        .transpose(2, 1, 0, 3)
        .reshape(PATCH, PATCH * channels, width)
    )
    bias = window_bias(token_cols)
    edge = jax.ShapeDtypeStruct((TOK_H * RADIUS, width), bf16)
    state = (
        jax.ShapeDtypeStruct((count, width), f32),
        jax.ShapeDtypeStruct((count, width), bf16),
        edge,
        edge,
    )
    stream, inputs, left, right = pl.pallas_call(
        functools.partial(merge_kernel, rows, token_cols),
        out_shape=state,
        in_specs=[SMEM, VMEM, VMEM, VMEM, VMEM],
        out_specs=(VMEM,) * 4,
        scratch_shapes=[
            pltpu.VMEM((tile_rows * channels, tile_cols), f32),
            pltpu.VMEM((tile_rows * channels, tile_cols), f32),
            pltpu.VMEM((TOK_H * tile_cols, PATCH * channels), f32),
        ],
        compiler_params=params,
        name="merge",
    )(meta, got, weights, embed, attn_gain[:1])
    halo = RADIUS * token_cols
    beside = (TOK_H + 2 * RADIUS) * RADIUS
    sizes = (lax.axis_size("row"), lax.axis_size("col"))
    hbm = pl.BlockSpec(memory_space=pl.ANY)
    for l in range(layers):
        last = l == layers - 1
        result = pl.pallas_call(
            functools.partial(layer_kernel, l, last, token_cols, sizes),
            out_shape=state[1] if last else state,
            in_specs=[VMEM, VMEM, VMEM, hbm, hbm, VMEM, VMEM, VMEM],
            out_specs=VMEM if last else (VMEM,) * 4,
            scratch_shapes=[
                pltpu.VMEM((count, width), bf16),
                pltpu.VMEM((count + 2 * halo, 2 * width), bf16),
                pltpu.VMEM((beside, 2 * width), bf16),
                pltpu.VMEM((beside, 2 * width), bf16),
                pltpu.VMEM((3, width, width), bf16),
                pltpu.VMEM((width, width), bf16),
                pltpu.VMEM((2 * halo, width), bf16),
                pltpu.VMEM((beside, width), bf16),
                pltpu.VMEM((beside, width), bf16),
                pltpu.SemaphoreType.DMA((4,)),
                pltpu.SemaphoreType.DMA((8,)),
                pltpu.SemaphoreType.DMA((8,)),
            ],
            compiler_params=pltpu.CompilerParams(
                vmem_limit_bytes=56 * 2**20, collective_id=l, has_side_effects=True
            ),
            name="layer" + str(l),
        )(
            inputs,
            left,
            right,
            qkv_weight,
            out_weight,
            stream,
            bias,
            attn_gain[min(l + 1, layers - 1)][None],
        )
        if last:
            return result.reshape(TOK_H, token_cols, width)
        stream, inputs, left, right = result


def solution(mesh):
    placed = (
        P(("row", "col"), None, None, None),
        P(("row", "col"), None),
        P(("row", "col")),
        P(("row", "col")),
        P(),
        P(),
        P(),
        P(),
        P(),
    )
    return jax.shard_map(
        per_device, mesh=mesh, in_specs=placed, out_specs=P("row", "col", None), check_vma=False
    )
```

time: 176 us -> 134 us (0.76); the launches traced: 173 us -> 133 us
  starting transfers between devices: 30.5 us -> 5.89 us
  Pallas kernels: 57.6 us -> 75.3 us
  waiting for transfers between devices: 59.4 us -> 44 us
  blocking collectives: 9.86 us -> 0 us
  other arithmetic: 7.07 us -> 2.15 us
  local copies, waits for them, and re-layouts: 8.65 us -> 5.95 us
    ppermute x8 -> x0, starting transfers between devices: 24.6 us -> none  [shifted(): return lax.ppermute(cells, axis, pairs)]
    ppermute x8 -> x0, waiting for transfers between devices: 18.8 us -> none  [shifted(): return lax.ppermute(cells, axis, pairs)]
    pallas_call x4, Pallas kernels: 57.6 us -> 75.3 us  [the longest x2 60.8 us: per_device(): pl.pallas_call(functools.partial(layer_kernel, l, last, token_cols, sizes...]
    all_to_all x1 -> x0, blocking collectives: 9.86 us -> none  [per_device(): got_meta = exchange(meta.reshape(device_count, capacity)).reshape(slots)]
    all_to_all x1, waiting for transfers between devices: 40.7 us -> 44 us  [per_device(): lax.all_to_all(payload, ('row', 'col'), split_axis=0, concat_axis=0, tile...]
    concatenate x2 -> x1, other arithmetic: 2.78 us -> 0.07 us  [window_bias(): jnp.concatenate([c % token_cols, s % RADIUS - RADIUS, s % RADIUS + token_...]
    slice x4 -> x0, local copies, waits for them, and re-layouts: 2.5 us -> none  [the longest x2 1.97 us: surround(): cells[TOK_H - RADIUS:]]
    reshape x2 -> x0, other arithmetic: 2.36 us -> none  [surround(): return (centre.reshape(-1, width), side.reshape(-1, width))]
  transfers between devices with their start and end apart: 9 -> 1, of which waited for: 9 -> 1; matrix products, arithmetic and copies ran while one was open for 3% -> 3% of each run, Pallas kernels for 0% -> 0%
where the time goes in v2:
time: 134 us; the launch traced here: 133 us
  Pallas kernels  75.3 us (56%)
  waiting for transfers between devices  44 us (33%)
  local copies, waits for them, and re-layouts  5.95 us (4%)
  starting transfers between devices  5.89 us (4%)
  other arithmetic  2.15 us (2%)
    pallas_call x2, Pallas kernels, per_device(): pl.pallas_call(functools.partial(layer_kernel, l, last, token_cols, sizes...  60.8 us
    all_to_all x1, waiting for transfers between devices, per_device(): lax.all_to_all(payload, ('row', 'col'), split_axis=0, concat_axis=0, tile...  44 us
    pallas_call x1, Pallas kernels, per_device(): pl.pallas_call(functools.partial(merge_kernel, rows, token_cols), out_sha...  10.3 us
    all_to_all x1, starting transfers between devices, per_device(): lax.all_to_all(payload, ('row', 'col'), split_axis=0, concat_axis=0, tile...  5.89 us
    pallas_call x1, Pallas kernels, per_device(): pl.pallas_call(functools.partial(place_kernel, capacity), out_shape=jax.S...  4.16 us
  transfers between devices with their start and end apart: 1, of which 1 were waited for; matrix products, arithmetic and copies ran while one was open for 3% of the time, Pallas kernels for 0%

profile of v2, /device:TPU:20, one launch (start us, length us, event | category | flops | bytes accessed | tf_op | source)
XLA Modules:
  0.0 133.4 jit_solution(7255000668596343171)
XLA Ops:
  0.0 0.0 copy-start
  0.0 4.2 %place.1 = bf16[32,272,128]{2,1,0:T(8,128)(2,1)} custom-call(s32[128]{0:T(128)} %bitcast.15, s32[128]{0:T(128)} %offsets.1, s32[128]{0:T(128)} %profile.1, f32[128,32,128]{2,1,0:T(8,128)} %bitcast.13), custom_call_target="tpu_custom_call" | custom-call | tf_op jit(solution)/shard_map/place/pallas_call | solution.py:319
  4.2 0.0 copy-start.2
  4.2 5.9 %all-to-all-start = ((bf16[32,272,128]{2,1,0:T(8,128)(2,1)}), bf16[32,272,128]{2,1,0:T(8,128)(2,1)S(1)}, u32[]{:S(2)}, u32[]{:S(2)}) async-start(bf16[32,272,128]{2,1,0:T(8,128)(2,1)} %place.1), calls=%async_computation | async-start | bytes 4456448 | tf_op jit(solution)/shard_map/all_to_all | solution.py:331
  10.1 0.0 copy-start.3
  10.1 0.0 copy-done.2
  10.1 1.5 %copy.14 = bf16[8,8,8,1024]{3,0,1,2:T(8,128)(2,1)} copy(bf16[8,8,8,1024]{3,2,1,0:T(8,128)(2,1)S(1)} %bitcast.14) | data formatting | bytes 2097152 | tf_op jit(solution)/shard_map/reshape | solution.py:340
  11.6 0.0 copy-done
  11.7 0.7 concatenate.20.weights
  12.4 0.1 add_compare_fusion.3
  12.5 0.1 pad_add_fusion
  12.6 0.1 add_add_fusion
  12.7 0.1 fusion.3
  12.8 0.0 copy-done.3
  12.8 0.6 fusion.6
  13.4 0.2 fusion
  13.6 1.0 and_select_fusion.bias
  14.5 44.0 %all-to-all-done.got = bf16[32,272,128]{2,1,0:T(8,128)(2,1)S(1)} async-done(((bf16[32,272,128]{2,1,0:T(8,128)(2,1)}), bf16[32,272,128]{2,1,0:T(8,128)(2,1)S(1)}, u32[]{:S(2)}, u32[]{:S(2)}) %all-to-all-start) | async-done | bytes 2228256 | tf_op jit(solution)/shard_map/all_to_all | solution.py:331
  58.5 0.0 copy-start.1
  58.5 0.7 convert_reduce_fusion
  59.2 0.7 convert_element_type.20.meta
  59.9 0.0 copy-done.1
  59.9 10.3 %merge.1 = (f32[512,1024]{1,0:T(8,128)}, bf16[512,1024]{1,0:T(8,128)(2,1)}, bf16[128,1024]{1,0:T(8,128)(2,1)}, bf16[128,1024]{1,0:T(8,128)(2,1)}) custom-call(s32[256]{0:T(256)} %convert_element_type.20.meta, bf16[32,272,128]{2,1,0:T(8,128)(2,1)} %copy-done.1, f32[17,32,128]{2,1,0:T(8,128)} %concatenate.20.weights, bf16[8,64,1024]{2,1,0:T(8,128)(2,1)} %bitcast.11, ...), custom_call_target="tpu_custom_call" | custom-call | tf_op jit(solution)/shard_map/merge/pallas_call | solution.py:352
  70.2 32.1 %layer0.1 = (f32[512,1024]{1,0:T(8,128)}, bf16[512,1024]{1,0:T(8,128)(2,1)}, bf16[128,1024]{1,0:T(8,128)(2,1)}, bf16[128,1024]{1,0:T(8,128)(2,1)}) custom-call(bf16[512,1024]{1,0:T(8,128)(2,1)} %get-tuple-element.13.x, bf16[128,1024]{1,0:T(8,128)(2,1)} %get-tuple-element.14.own_left, bf16[128,1024]{1,0:T(8,128)(2,1)} %get-tuple-element.15.own_right, ...), custom_call_target="tpu_custom_call" | custom-call | tf_op jit(solution)/shard_map/layer0/pallas_call | solution.py:371
  102.4 28.7 %layer1.1 = bf16[512,1024]{1,0:T(8,128)(2,1)} custom-call(bf16[512,1024]{1,0:T(8,128)(2,1)} %get-tuple-element.17.x, bf16[128,1024]{1,0:T(8,128)(2,1)} %get-tuple-element.18.own_left, bf16[128,1024]{1,0:T(8,128)(2,1)} %get-tuple-element.19.own_right, bf16[2,1024,3072]{2,1,0:T(8,128)(2,1)} %qkv.3, bf16[2,1024,1024]{2,1,0:T(8,128)(2,1)} %out_w.3, ...), custom_call_target="tpu_custom_call" | custom-call | tf_op jit(solution)/shard_map/layer1/pallas_call | solution.py:371
  131.1 2.3 %copy.16 = bf16[32,16,1024]{2,1,0:T(8,128)(2,1)} copy(bf16[32,16,1024]{2,1,0:T(8,128)(2,1)} %bitcast.12) | data formatting | bytes 2097152
  (7 shorter events, 0.0 us)
Async XLA Ops:
  0.0 11.6 %copy-start = (f32[16,4,128]{2,1,0:T(4,128)S(1)}, f32[16,4,128]{2,1,0:T(4,128)}, u32[]{:S(2)}) copy-start(f32[16,4,128]{2,1,0:T(4,128)} %param.13) | copy-start | bytes 98308
  4.2 5.9 %copy-start.2 = (bf16[512,1024]{1,0:T(8,128)(2,1)S(1)}, bf16[512,1024]{1,0:T(8,128)(2,1)}, u32[]{:S(2)}) copy-start(bf16[512,1024]{1,0:T(8,128)(2,1)} %param.14) | copy-start | bytes 3145732
  4.2 54.4 %all-to-all-start = ((bf16[32,272,128]{2,1,0:T(8,128)(2,1)}), bf16[32,272,128]{2,1,0:T(8,128)(2,1)S(1)}, u32[]{:S(2)}, u32[]{:S(2)}) async-start(bf16[32,272,128]{2,1,0:T(8,128)(2,1)} %place.1), calls=%async_computation | async-start | bytes 4456448 | tf_op jit(solution)/shard_map/all_to_all | solution.py:331
  10.1 2.7 %copy-start.3 = (f32[2,1024]{1,0:T(2,128)S(1)}, f32[2,1024]{1,0:T(2,128)}, u32[]{:S(2)}) copy-start(f32[2,1024]{1,0:T(2,128)} %param.15) | copy-start | bytes 24580
  58.5 1.4 %copy-start.1 = (bf16[32,272,128]{2,1,0:T(8,128)(2,1)}, bf16[32,272,128]{2,1,0:T(8,128)(2,1)S(1)}, u32[]{:S(2)}) copy-start(bf16[32,272,128]{2,1,0:T(8,128)(2,1)S(1)} %all-to-all-done.got) | copy-start | bytes 6684676

commit v3 on v2

v3 whole, which is shorter than its diff:
```python
import functools

import jax
import jax.numpy as jnp
from jax import lax
from jax.experimental import pallas as pl
from jax.experimental.pallas import tpu as pltpu
from jax.sharding import PartitionSpec as P

HEADS = 16
RADIUS = 4
TOK_H = 32
PATCH = 8
BAND = 8

VMEM = pl.BlockSpec(memory_space=pltpu.VMEM)
SMEM = pl.BlockSpec(memory_space=pltpu.SMEM)


def place_kernel(capacity, dest, offsets, profile, scans, payload, index, count):
    blocks, rows, lanes = scans.shape
    tiles = payload.shape[0]
    payload[...] = jnp.zeros_like(payload)
    index[...] = jnp.zeros_like(index)
    first = lax.broadcasted_iota(jnp.int32, (1, lanes), 1) < lanes // 2

    def clear(i, c):
        count[i] = 0
        return c

    lax.fori_loop(0, tiles, clear, 0, unroll=8)

    def put(b, c):
        tile = dest[b]
        rank = count[tile]
        count[tile] = rank + 1
        payload[tile, pl.ds(pl.multiple_of(rank * rows, rows), rows), :] = scans[b].astype(
            jnp.bfloat16
        )
        named = jnp.where(first, offsets[b], profile[b] + 1).astype(jnp.float32)
        index[tile, pl.ds(rank, 1), :] = named
        return c

    lax.fori_loop(0, blocks, put, 0, unroll=4)
    payload[:, capacity * rows :, :] = index[...].astype(jnp.bfloat16)


def normed(stream, gain_row):
    centre = jnp.mean(stream, -1, keepdims=True)
    spread = jnp.mean(jnp.square(stream - centre), -1, keepdims=True)
    return ((stream - centre) * lax.rsqrt(spread + 1e-05) * gain_row).astype(jnp.bfloat16)


def regroup(token_cols, back=False):
    tokens = BAND * token_cols
    each = BAND * RADIUS
    shape = (tokens, tokens)
    grouped = lax.broadcasted_iota(jnp.int32, shape, 1 if back else 0)
    natural = lax.broadcasted_iota(jnp.int32, shape, 0 if back else 1)
    inner = grouped % each
    source = inner // RADIUS * token_cols + grouped // each * RADIUS + inner % RADIUS
    return (natural == source).astype(jnp.float32).astype(jnp.bfloat16)


def store_band(b, total, cells, stream, inputs):
    each = BAND * RADIUS
    units = each // inputs.shape[2]
    at = pl.ds(pl.multiple_of(b * each, each), each)
    for g in range(inputs.shape[0]):
        rows = slice(g * each, (g + 1) * each)
        stream[g, at, :] = total[rows]
        inputs[g, pl.ds(b * units, units)] = cells[rows].reshape(
            units, each // units, cells.shape[1]
        )


def merge_kernel(
    rows, token_cols, meta, got, weights, embed, gain, stream, inputs, num, den, turned
):
    tiles, _, lanes = got.shape
    capacity = meta.shape[0] // tiles
    num[...] = jnp.zeros_like(num)
    den[...] = jnp.ones_like(den)

    def add_tile(t, c):
        for r in range(capacity):
            m = meta[t * capacity + r]
            w = weights[m >> 8]
            at = pl.ds(pl.multiple_of((m & 255) * 8, 8), rows)
            num[at, :] += got[t, r * rows : (r + 1) * rows, :].astype(jnp.float32) * w
            den[at, :] += w
        return c

    lax.fori_loop(0, tiles, add_tile, 0)
    group = PATCH * 8

    def turn(i, c):
        at = pl.ds(pl.multiple_of(i * group, group), group)
        merged = (num[at, :] / den[at, :]).astype(jnp.bfloat16).astype(jnp.float32)
        turned[pl.ds(pl.multiple_of(i * lanes, lanes), lanes), :] = merged.T
        return c

    lax.fori_loop(0, TOK_H, turn, 0, unroll=4)
    part = BAND * token_cols
    order = regroup(token_cols)

    def embed_part(k, c):
        total = None
        for q in range(PATCH):
            lhs = turned[pl.ds(k * part * PATCH + q, part, stride=PATCH), :]
            lhs = jnp.dot(order, lhs.astype(jnp.bfloat16), preferred_element_type=jnp.float32)
            term = jnp.dot(
                lhs.astype(jnp.bfloat16), embed[q], preferred_element_type=jnp.float32
            )
            total = term if total is None else total + term
        store_band(k, total, normed(total, gain[...]), stream, inputs)
        return c

    lax.fori_loop(0, TOK_H // BAND, embed_part, 0)


def layer_kernel(layer, last, token_cols, sizes, x, qkv, out_w, stream, bias, gain, *refs):
    outs, refs = (refs[:1], refs[1:]) if last else (refs[:2], refs[2:])
    q_ref, kv, w, wo, xh, w_sem, send, recv = refs
    width = wo.shape[0]
    head_dim = width // HEADS
    groups, units, unit, _ = x.shape
    own = units * unit
    count = groups * own
    loads = [
        pltpu.make_async_copy(
            qkv.at[layer, :, n * width : (n + 1) * width], w.at[n], w_sem.at[n]
        )
        for n in range(3)
    ] + [pltpu.make_async_copy(out_w.at[layer], wo, w_sem.at[3])]
    for load in loads:
        load.start()

    row, col = lax.axis_index("row"), lax.axis_index("col")
    up, down = row > 0, row < sizes[0] - 1
    west, east = col > 0, col < sizes[1] - 1
    top, bottom = xh.at[:groups], xh.at[groups : 2 * groups]
    l0 = 2 * groups
    r0 = l0 + units + 2
    end = r0 + units + 2
    moves = [
        (-1, 0, up, x.at[:, 0], bottom, top),
        (1, 0, down, x.at[:, units - 1], top, bottom),
        (0, -1, west, x.at[0], xh.at[r0 + 1 : end - 1], xh.at[l0 + 1 : r0 - 1]),
        (0, 1, east, x.at[groups - 1], xh.at[l0 + 1 : r0 - 1], xh.at[r0 + 1 : end - 1]),
        (-1, -1, up & west, x.at[0, 0], xh.at[end - 1], xh.at[l0]),
        (-1, 1, up & east, x.at[groups - 1, 0], xh.at[r0 - 1], xh.at[r0]),
        (1, -1, down & west, x.at[0, units - 1], xh.at[r0], xh.at[r0 - 1]),
        (1, 1, down & east, x.at[groups - 1, units - 1], xh.at[l0], xh.at[end - 1]),
    ]
    opposite = [1, 0, 3, 2, 7, 6, 5, 4]
    barrier = pltpu.get_barrier_semaphore()
    mesh_ids = pl.DeviceIdType.MESH
    for dr, dc, there, _, _, _ in moves:

        @pl.when(there)
        def _(dr=dr, dc=dc):
            pl.semaphore_signal(
                barrier, inc=1, device_id=(row + dr, col + dc), device_id_type=mesh_ids
            )

    for _, _, there, _, _, here in moves:

        @pl.when(jnp.logical_not(there))
        def _(here=here):
            here[...] = jnp.zeros(here.shape, here.dtype)

    rows_near = 1 + up.astype(jnp.int32) + down.astype(jnp.int32)
    cols_near = 1 + west.astype(jnp.int32) + east.astype(jnp.int32)
    pl.semaphore_wait(barrier, rows_near * cols_near - 1)
    copies = []
    for n, (dr, dc, there, source, lands, _) in enumerate(moves):
        copies.append(
            pltpu.make_async_remote_copy(
                src_ref=source,
                dst_ref=lands,
                send_sem=send.at[n],
                recv_sem=recv.at[n],
                device_id=(row + dr, col + dc),
                device_id_type=mesh_ids,
            )
        )

        @pl.when(there)
        def _(copy=copies[-1]):
            copy.start()

    step = 512

    def project(n, put):
        rows = x if n < 3 else xh
        weight = w.at[n] if n < 3 else w.at[n - 2]
        total = count if n < 3 else end * unit

        def part(k, c):
            cols = pl.ds(pl.multiple_of(k * step, step), step)
            y = jnp.dot(
                rows[...].reshape(total, width),
                weight[:, cols],
                preferred_element_type=jnp.float32,
            ).astype(jnp.bfloat16)
            put(k, y)
            return c

        lax.fori_loop(0, width // step, part, 0)

    def put_q(k, y):
        cols = pl.ds(pl.multiple_of(k * step, step), step)
        for g in range(groups):
            q_ref[g, :, cols] = (y[g * own : (g + 1) * own] * head_dim ** (-0.5)).astype(
                jnp.bfloat16
            )

    def put_own(base, k, y):
        cols = pl.ds(pl.multiple_of(base + k * step, step), step)
        for g in range(groups):
            kv[g + 1, unit : unit + own, cols] = y[g * own : (g + 1) * own]

    def put_halo(base, k, y):
        cols = pl.ds(pl.multiple_of(base + k * step, step), step)
        for g in range(groups):
            kv[g + 1, :unit, cols] = y[g * unit : (g + 1) * unit]
            kv[g + 1, unit + own :, cols] = y[(groups + g) * unit : (groups + g + 1) * unit]
        kv[0, :, cols] = y[l0 * unit : r0 * unit]
        kv[groups + 1, :, cols] = y[r0 * unit :]

    loads[0].wait()
    project(0, put_q)
    for n in (1, 2):
        loads[n].wait()
        project(n, functools.partial(put_own, (n - 1) * width))
    for n, (_, _, there, _, _, here) in enumerate(moves):

        @pl.when(there)
        def _(n=n, here=here):
            copies[n].wait_send()
            pltpu.make_async_remote_copy(
                src_ref=here,
                dst_ref=here,
                send_sem=send.at[n],
                recv_sem=recv.at[opposite[n]],
                device_id=(row + moves[n][0], col + moves[n][1]),
                device_id_type=mesh_ids,
            ).wait_recv()

    for n in (3, 4):
        project(n, functools.partial(put_halo, (n - 3) * width))
    loads[3].wait()
    each = BAND * RADIUS
    span = (BAND + 2 * RADIUS) * RADIUS
    pair = 2 * head_dim
    queries = 2 * each
    low = lax.broadcasted_iota(jnp.int32, (queries, pair), 1) < head_dim
    ones = jnp.ones((4 * span, pair), jnp.bfloat16)
    order = regroup(token_cols, True) if last else None

    def band(b, carry):
        q_at = pl.ds(pl.multiple_of(b * each, each), each)
        k_at = pl.ds(pl.multiple_of(b * each, each), span)
        halves = []
        for s in range(groups // 2):
            half_bias = bias[b, s]
            both = jnp.concatenate([half_bias, half_bias], 0)
            pieces = []
            for h in range(HEADS // 2):
                cols = slice(h * pair, (h + 1) * pair)
                v_cols = slice(width + h * pair, width + (h + 1) * pair)
                q = jnp.concatenate([q_ref[2 * s + i, q_at, cols] for i in range(2)], 0)
                zero = jnp.zeros_like(q)
                q2 = jnp.concatenate([jnp.where(low, q, zero), jnp.where(low, zero, q)], 0)
                k = jnp.concatenate([kv[2 * s + i, k_at, cols] for i in range(4)], 0)
                v = jnp.concatenate([kv[2 * s + i, k_at, v_cols] for i in range(4)], 0)
                logits = lax.dot_general(
                    q2, k, (((1,), (1,)), ((), ())), preferred_element_type=jnp.float32
                )
                logits = logits + both
                top_logit = jnp.max(logits, -1, keepdims=True)
                weight = jnp.exp(logits - top_logit).astype(jnp.bfloat16)
                summed = jnp.dot(
                    weight, jnp.concatenate([v, ones], 1), preferred_element_type=jnp.float32
                )
                share = summed[:, :pair] / summed[:, pair:]
                pieces.append(
                    jnp.where(low, share[:queries], share[queries:]).astype(jnp.bfloat16)
                )
            halves.append(jnp.concatenate(pieces, 1))
        attended = jnp.concatenate(halves, 0)
        before = jnp.concatenate([stream[g, q_at, :] for g in range(groups)], 0)
        total = before + jnp.dot(attended, wo[...], preferred_element_type=jnp.float32)
        if last:
            rows = BAND * token_cols
            outs[0][pl.ds(pl.multiple_of(b * rows, rows), rows), :] = jnp.dot(
                order, total.astype(jnp.bfloat16), preferred_element_type=jnp.float32
            ).astype(jnp.bfloat16)
        else:
            store_band(b, total, normed(total, gain[...]), outs[0], outs[1])
        return carry

    lax.fori_loop(0, TOK_H // BAND, band, 0)


def window_bias(token_cols):
    bands, halves = TOK_H // BAND, token_cols // (2 * RADIUS)
    win = BAND + 2 * RADIUS
    q = jnp.arange(2 * BAND * RADIUS, dtype=jnp.int32)
    k = jnp.arange(4 * win * RADIUS, dtype=jnp.int32)
    q_row = q % (BAND * RADIUS) // RADIUS
    q_col = q // (BAND * RADIUS) * RADIUS + q % RADIUS
    k_row = k % (win * RADIUS) // RADIUS - RADIUS
    k_col = k // (win * RADIUS) * RADIUS + k % RADIUS - RADIUS
    near = (jnp.abs(k_row[None] - q_row[:, None]) <= RADIUS) & (
        jnp.abs(k_col[None] - q_col[:, None]) <= RADIUS
    )
    g_row = (
        lax.axis_index("row") * TOK_H
        + jnp.arange(bands, dtype=jnp.int32)[:, None] * BAND
        + k_row[None]
    )
    g_col = (
        lax.axis_index("col") * token_cols
        + jnp.arange(halves, dtype=jnp.int32)[:, None] * 2 * RADIUS
        + k_col[None]
    )
    row_in = (g_row >= 0) & (g_row < TOK_H * lax.axis_size("row"))
    col_in = (g_col >= 0) & (g_col < token_cols * lax.axis_size("col"))
    inside = row_in[:, None] & col_in[None]
    return jnp.where(near[None, None] & inside[:, :, None], 0.0, -1e30).astype(jnp.float32)


def per_device(
    scans, dest, offsets, profile_index, profiles, embed_weight, attn_gain, qkv_weight, out_weight
):
    device_count = lax.axis_size("row") * lax.axis_size("col")
    blocks, strip_rows, channels, tile_cols = scans.shape
    token_cols = tile_cols // PATCH
    count = TOK_H * token_cols
    tile_rows = TOK_H * PATCH
    profile_count = profiles.shape[0]
    width = embed_weight.shape[1]
    layers = qkv_weight.shape[0]
    capacity = max(2, 2 * blocks // device_count)
    slots = device_count * capacity
    rows = strip_rows * channels
    extra = -(-capacity // 16) * 16
    f32, bf16 = jnp.float32, jnp.bfloat16
    params = pltpu.CompilerParams(vmem_limit_bytes=56 * 2**20)

    payload = pl.pallas_call(
        functools.partial(place_kernel, capacity),
        out_shape=jax.ShapeDtypeStruct((device_count, capacity * rows + extra, tile_cols), bf16),
        in_specs=[SMEM, SMEM, SMEM, VMEM],
        out_specs=VMEM,
        scratch_shapes=[
            pltpu.VMEM((device_count, extra, tile_cols), f32),
            pltpu.SMEM((device_count,), jnp.int32),
        ],
        compiler_params=params,
        name="place",
    )(dest[:, 0], offsets, profile_index, scans.reshape(blocks, rows, tile_cols))
    got = lax.all_to_all(payload, ("row", "col"), split_axis=0, concat_axis=0, tiled=True)
    named = got[:, capacity * rows : capacity * rows + capacity, :]
    meta = (named[:, :, 0] + named[:, :, tile_cols // 2].astype(f32) * 256.0).astype(jnp.int32)
    meta = meta.reshape(slots)
    weights = jnp.broadcast_to(
        profiles[:, :, None, :], (profile_count, strip_rows, channels, tile_cols)
    ).reshape(profile_count, rows, tile_cols)
    weights = jnp.concatenate([jnp.zeros((1, rows, tile_cols), f32), weights], 0)
    embed = (
        embed_weight.reshape(channels, PATCH, PATCH, width)
        .transpose(2, 1, 0, 3)
        .reshape(PATCH, PATCH * channels, width)
    )
    bias = window_bias(token_cols)
    groups = token_cols // RADIUS
    unit = RADIUS * RADIUS
    units = TOK_H // RADIUS
    state = (
        jax.ShapeDtypeStruct((groups, units * unit, width), f32),
        jax.ShapeDtypeStruct((groups, units, unit, width), bf16),
    )
    stream, inputs = pl.pallas_call(
        functools.partial(merge_kernel, rows, token_cols),
        out_shape=state,
        in_specs=[SMEM, VMEM, VMEM, VMEM, VMEM],
        out_specs=(VMEM,) * 2,
        scratch_shapes=[
            pltpu.VMEM((tile_rows * channels, tile_cols), f32),
            pltpu.VMEM((tile_rows * channels, tile_cols), f32),
            pltpu.VMEM((TOK_H * tile_cols, PATCH * channels), f32),
        ],
        compiler_params=params,
        name="merge",
    )(meta, got, weights, embed, attn_gain[:1])
    sizes = (lax.axis_size("row"), lax.axis_size("col"))
    hbm = pl.BlockSpec(memory_space=pl.ANY)
    for l in range(layers):
        last = l == layers - 1
        result = pl.pallas_call(
            functools.partial(layer_kernel, l, last, token_cols, sizes),
            out_shape=jax.ShapeDtypeStruct((count, width), bf16) if last else state,
            in_specs=[VMEM, hbm, hbm, VMEM, VMEM, VMEM],
            out_specs=VMEM if last else (VMEM,) * 2,
            scratch_shapes=[
                pltpu.VMEM((groups, units * unit, width), bf16),
                pltpu.VMEM((groups + 2, (units + 2) * unit, 2 * width), bf16),
                pltpu.VMEM((3, width, width), bf16),
                pltpu.VMEM((width, width), bf16),
                pltpu.VMEM((2 * groups + 2 * (units + 2), unit, width), bf16),
                pltpu.SemaphoreType.DMA((4,)),
                pltpu.SemaphoreType.DMA((8,)),
                pltpu.SemaphoreType.DMA((8,)),
            ],
            compiler_params=pltpu.CompilerParams(
                vmem_limit_bytes=56 * 2**20, collective_id=l, has_side_effects=True
            ),
            name="layer" + str(l),
        )(
            inputs,
            qkv_weight,
            out_weight,
            stream,
            bias,
            attn_gain[min(l + 1, layers - 1)][None],
        )
        if last:
            return result.reshape(TOK_H, token_cols, width)
        stream, inputs = result


def solution(mesh):
    placed = (
        P(("row", "col"), None, None, None),
        P(("row", "col"), None),
        P(("row", "col")),
        P(("row", "col")),
        P(),
        P(),
        P(),
        P(),
        P(),
    )
    return jax.shard_map(
        per_device, mesh=mesh, in_specs=placed, out_specs=P("row", "col", None), check_vma=False
    )
```

time: 134 us -> 123 us (0.918)
  Pallas kernels: 75.3 us -> 63.6 us
    pallas_call x2, Pallas kernels: 60.8 us -> 45.9 us  [per_device(): pl.pallas_call(functools.partial(layer_kernel, l, last, token_cols, sizes...]
    pallas_call x1, Pallas kernels: 10.3 us -> 13.5 us  [per_device(): pl.pallas_call(functools.partial(merge_kernel, rows, token_cols), out_sha...]
where the time goes in v3:
time: 123 us; the launch traced here: 122 us
  Pallas kernels  63.6 us (52%)
  waiting for transfers between devices  44.3 us (36%)
  local copies, waits for them, and re-layouts  5.93 us (5%)
  starting transfers between devices  5.89 us (5%)
  other arithmetic  1.84 us (1%)
    pallas_call x2, Pallas kernels, per_device(): pl.pallas_call(functools.partial(layer_kernel, l, last, token_cols, sizes...  45.9 us
    all_to_all x1, waiting for transfers between devices, per_device(): lax.all_to_all(payload, ('row', 'col'), split_axis=0, concat_axis=0, tile...  44.3 us
    pallas_call x1, Pallas kernels, per_device(): pl.pallas_call(functools.partial(merge_kernel, rows, token_cols), out_sha...  13.5 us
    all_to_all x1, starting transfers between devices, per_device(): lax.all_to_all(payload, ('row', 'col'), split_axis=0, concat_axis=0, tile...  5.89 us
    pallas_call x1, Pallas kernels, per_device(): pl.pallas_call(functools.partial(place_kernel, capacity), out_shape=jax.S...  4.14 us
  transfers between devices with their start and end apart: 1, of which 1 were waited for; matrix products, arithmetic and copies ran while one was open for 3% of the time, Pallas kernels for 0%

profile of v3, /device:TPU:20, one launch (start us, length us, event | category | flops | bytes accessed | tf_op | source)
XLA Modules:
  0.0 121.6 jit_solution(15019654972476704594)
XLA Ops:
  0.0 0.0 copy-start
  0.0 4.1 %place.1 = bf16[32,272,128]{2,1,0:T(8,128)(2,1)} custom-call(s32[128]{0:T(128)} %bitcast.15, s32[128]{0:T(128)} %offsets.1, s32[128]{0:T(128)} %profile.1, f32[128,32,128]{2,1,0:T(8,128)} %bitcast.13), custom_call_target="tpu_custom_call" | custom-call | tf_op jit(solution)/shard_map/place/pallas_call | solution.py:353
  4.1 0.0 copy-start.2
  4.2 5.9 %all-to-all-start = ((bf16[32,272,128]{2,1,0:T(8,128)(2,1)}), bf16[32,272,128]{2,1,0:T(8,128)(2,1)S(1)}, u32[]{:S(2)}, u32[]{:S(2)}) async-start(bf16[32,272,128]{2,1,0:T(8,128)(2,1)} %place.1), calls=%async_computation | async-start | bytes 4456448 | tf_op jit(solution)/shard_map/all_to_all | solution.py:365
  10.1 0.0 copy-start.3
  10.1 0.0 copy-done.2
  10.1 1.5 %copy.14 = bf16[8,8,8,1024]{3,0,1,2:T(8,128)(2,1)} copy(bf16[8,8,8,1024]{3,2,1,0:T(8,128)(2,1)S(1)} %bitcast.14) | data formatting | bytes 2097152 | tf_op jit(solution)/shard_map/reshape | solution.py:374
  11.6 0.0 copy-done
  11.7 0.8 concatenate.3.weights
  12.4 0.1 compare_and_fusion
  12.5 0.1 fusion.1
  12.6 0.0 copy-done.3
  12.6 0.6 fusion.9
  13.2 0.1 fusion
  13.3 0.9 and_select_fusion.bias
  14.2 44.3 %all-to-all-done.got = bf16[32,272,128]{2,1,0:T(8,128)(2,1)S(1)} async-done(((bf16[32,272,128]{2,1,0:T(8,128)(2,1)}), bf16[32,272,128]{2,1,0:T(8,128)(2,1)S(1)}, u32[]{:S(2)}, u32[]{:S(2)}) %all-to-all-start) | async-done | bytes 2228256 | tf_op jit(solution)/shard_map/all_to_all | solution.py:365
  58.5 0.0 copy-start.1
  58.5 0.7 convert_reduce_fusion
  59.2 0.7 convert_element_type.20.meta
  59.9 0.0 copy-done.1
  59.9 13.5 %merge.1 = (f32[4,128,1024]{2,1,0:T(8,128)}, bf16[4,8,16,1024]{3,2,1,0:T(8,128)(2,1)}) custom-call(s32[256]{0:T(256)} %convert_element_type.20.meta, bf16[32,272,128]{2,1,0:T(8,128)(2,1)} %copy-done.1, f32[17,32,128]{2,1,0:T(8,128)} %concatenate.3.weights, bf16[8,64,1024]{2,1,0:T(8,128)(2,1)} %bitcast.11, f32[1,1024]{1,0:T(1,128)} %get-tuple-element.14.gain), custom_call_target="tpu_custom_call" | custom-call | tf_op jit(solution)/shard_map/merge/pallas_call | solution.py:386
  73.4 24.3 %layer0.1 = (f32[4,128,1024]{2,1,0:T(8,128)}, bf16[4,8,16,1024]{3,2,1,0:T(8,128)(2,1)}) custom-call(bf16[4,8,16,1024]{3,2,1,0:T(8,128)(2,1)} %get-tuple-element.9.x, bf16[2,1024,3072]{2,1,0:T(8,128)(2,1)} %qkv.3, bf16[2,1024,1024]{2,1,0:T(8,128)(2,1)} %out_w.3, f32[4,128,1024]{2,1,0:T(8,128)} %get-tuple-element.10.stream, ...), custom_call_target="tpu_custom_call" | custom-call | tf_op jit(solution)/shard_map/layer0/pallas_call | solution.py:403
  97.7 21.6 %layer1.1 = bf16[512,1024]{1,0:T(8,128)(2,1)} custom-call(bf16[4,8,16,1024]{3,2,1,0:T(8,128)(2,1)} %get-tuple-element.11.x, bf16[2,1024,3072]{2,1,0:T(8,128)(2,1)} %qkv.3, bf16[2,1024,1024]{2,1,0:T(8,128)(2,1)} %out_w.3, f32[4,128,1024]{2,1,0:T(8,128)} %get-tuple-element.12.stream, f32[4,2,64,256]{3,2,1,0:T(8,128)} %and_select_fusion.bias, ...), custom_call_target="tpu_custom_call" | custom-call | tf_op jit(solution)/shard_map/layer1/pallas_call | solution.py:403
  119.3 2.3 %copy.16 = bf16[32,16,1024]{2,1,0:T(8,128)(2,1)} copy(bf16[32,16,1024]{2,1,0:T(8,128)(2,1)} %bitcast.12) | data formatting | bytes 2097152
  (6 shorter events, 0.1 us)
Async XLA Ops:
  0.0 11.6 %copy-start = (f32[16,4,128]{2,1,0:T(4,128)S(1)}, f32[16,4,128]{2,1,0:T(4,128)}, u32[]{:S(2)}) copy-start(f32[16,4,128]{2,1,0:T(4,128)} %param.13) | copy-start | bytes 98308
  4.1 5.9 %copy-start.2 = (bf16[512,1024]{1,0:T(8,128)(2,1)S(1)}, bf16[512,1024]{1,0:T(8,128)(2,1)}, u32[]{:S(2)}) copy-start(bf16[512,1024]{1,0:T(8,128)(2,1)} %param.14) | copy-start | bytes 3145732
  4.2 54.4 %all-to-all-start = ((bf16[32,272,128]{2,1,0:T(8,128)(2,1)}), bf16[32,272,128]{2,1,0:T(8,128)(2,1)S(1)}, u32[]{:S(2)}, u32[]{:S(2)}) async-start(bf16[32,272,128]{2,1,0:T(8,128)(2,1)} %place.1), calls=%async_computation | async-start | bytes 4456448 | tf_op jit(solution)/shard_map/all_to_all | solution.py:365
  10.1 2.6 %copy-start.3 = (f32[2,1024]{1,0:T(2,128)S(1)}, f32[2,1024]{1,0:T(2,128)}, u32[]{:S(2)}) copy-start(f32[2,1024]{1,0:T(2,128)} %param.15) | copy-start | bytes 24580
  58.5 1.4 %copy-start.1 = (bf16[32,272,128]{2,1,0:T(8,128)(2,1)}, bf16[32,272,128]{2,1,0:T(8,128)(2,1)S(1)}, u32[]{:S(2)}) copy-start(bf16[32,272,128]{2,1,0:T(8,128)(2,1)S(1)} %all-to-all-done.got) | copy-start | bytes 6684676

commit v4 on v3

--- a/solution.py
+++ b/solution.py
@@ -105,14 +105,12 @@
     order = regroup(token_cols)
 
     def embed_part(k, c):
-        total = None
-        for q in range(PATCH):
-            lhs = turned[pl.ds(k * part * PATCH + q, part, stride=PATCH), :]
-            lhs = jnp.dot(order, lhs.astype(jnp.bfloat16), preferred_element_type=jnp.float32)
-            term = jnp.dot(
-                lhs.astype(jnp.bfloat16), embed[q], preferred_element_type=jnp.float32
-            )
-            total = term if total is None else total + term
+        parts = [
+            turned[pl.ds(k * part * PATCH + q, part, stride=PATCH), :] for q in range(PATCH)
+        ]
+        lhs = jnp.concatenate(parts, 1).astype(jnp.bfloat16)
+        lhs = jnp.dot(order, lhs, preferred_element_type=jnp.float32).astype(jnp.bfloat16)
+        total = jnp.dot(lhs, embed[...], preferred_element_type=jnp.float32)
         store_band(k, total, normed(total, gain[...]), stream, inputs)
         return c
 
@@ -373,7 +371,7 @@
     embed = (
         embed_weight.reshape(channels, PATCH, PATCH, width)
         .transpose(2, 1, 0, 3)
-        .reshape(PATCH, PATCH * channels, width)
+        .reshape(PATCH * PATCH * channels, width)
     )
     bias = window_bias(token_cols)
     groups = token_cols // RADIUS

time: 123 us -> 118 us (0.959)
  Pallas kernels: 63.6 us -> 59.4 us
    pallas_call x1, Pallas kernels: 13.5 us -> 8.98 us  [per_device(): pl.pallas_call(functools.partial(merge_kernel, rows, token_cols), out_sha...]
where the time goes in v4:
time: 118 us; the launch traced here: 117 us
  Pallas kernels  59.4 us (50%)
  waiting for transfers between devices  44.3 us (38%)
  local copies, waits for them, and re-layouts  5.93 us (5%)
  starting transfers between devices  5.89 us (5%)
  other arithmetic  1.84 us (2%)
    pallas_call x2, Pallas kernels, per_device(): pl.pallas_call(functools.partial(layer_kernel, l, last, token_cols, sizes...  46.3 us
    all_to_all x1, waiting for transfers between devices, per_device(): lax.all_to_all(payload, ('row', 'col'), split_axis=0, concat_axis=0, tile...  44.3 us
    pallas_call x1, Pallas kernels, per_device(): pl.pallas_call(functools.partial(merge_kernel, rows, token_cols), out_sha...  8.98 us
    all_to_all x1, starting transfers between devices, per_device(): lax.all_to_all(payload, ('row', 'col'), split_axis=0, concat_axis=0, tile...  5.89 us
    pallas_call x1, Pallas kernels, per_device(): pl.pallas_call(functools.partial(place_kernel, capacity), out_shape=jax.S...  4.14 us
  transfers between devices with their start and end apart: 1, of which 1 were waited for; matrix products, arithmetic and copies ran while one was open for 3% of the time, Pallas kernels for 0%

profile of v4, /device:TPU:20, one launch (start us, length us, event | category | flops | bytes accessed | tf_op | source)
XLA Modules:
  0.0 117.5 jit_solution(14642333793877700631)
XLA Ops:
  0.0 0.0 copy-start
  0.0 4.1 %place.1 = bf16[32,272,128]{2,1,0:T(8,128)(2,1)} custom-call(s32[128]{0:T(128)} %bitcast.13, s32[128]{0:T(128)} %offsets.1, s32[128]{0:T(128)} %profile.1, f32[128,32,128]{2,1,0:T(8,128)} %bitcast.11), custom_call_target="tpu_custom_call" | custom-call | tf_op jit(solution)/shard_map/place/pallas_call | solution.py:351
  4.1 0.0 copy-start.2
  4.2 5.9 %all-to-all-start = ((bf16[32,272,128]{2,1,0:T(8,128)(2,1)}), bf16[32,272,128]{2,1,0:T(8,128)(2,1)S(1)}, u32[]{:S(2)}, u32[]{:S(2)}) async-start(bf16[32,272,128]{2,1,0:T(8,128)(2,1)} %place.1), calls=%async_computation | async-start | bytes 4456448 | tf_op jit(solution)/shard_map/all_to_all | solution.py:363
  10.1 0.0 copy-start.3
  10.1 0.0 copy-done.2
  10.1 1.5 %copy.12 = bf16[8,8,8,1024]{3,0,1,2:T(8,128)(2,1)} copy(bf16[8,8,8,1024]{3,2,1,0:T(8,128)(2,1)S(1)} %bitcast.12) | data formatting | bytes 2097152 | tf_op jit(solution)/shard_map/reshape | solution.py:372
  11.6 0.0 copy-done
  11.7 0.8 concatenate.3.weights
  12.4 0.1 compare_and_fusion
  12.5 0.1 fusion.1
  12.6 0.0 copy-done.3
  12.6 0.6 fusion.9
  13.2 0.1 fusion
  13.3 0.9 and_select_fusion.bias
  14.2 44.3 %all-to-all-done.got = bf16[32,272,128]{2,1,0:T(8,128)(2,1)S(1)} async-done(((bf16[32,272,128]{2,1,0:T(8,128)(2,1)}), bf16[32,272,128]{2,1,0:T(8,128)(2,1)S(1)}, u32[]{:S(2)}, u32[]{:S(2)}) %all-to-all-start) | async-done | bytes 2228256 | tf_op jit(solution)/shard_map/all_to_all | solution.py:363
  58.5 0.0 copy-start.1
  58.5 0.7 convert_reduce_fusion
  59.2 0.7 convert_element_type.20.meta
  59.9 0.0 copy-done.1
  59.9 9.0 %merge.1 = (f32[4,128,1024]{2,1,0:T(8,128)}, bf16[4,8,16,1024]{3,2,1,0:T(8,128)(2,1)}) custom-call(s32[256]{0:T(256)} %convert_element_type.20.meta, bf16[32,272,128]{2,1,0:T(8,128)(2,1)} %copy-done.1, f32[17,32,128]{2,1,0:T(8,128)} %concatenate.3.weights, bf16[512,1024]{1,0:T(8,128)(2,1)} %bitcast.9, f32[1,1024]{1,0:T(1,128)} %get-tuple-element.14.gain), custom_call_target="tpu_custom_call" | custom-call | tf_op jit(solution)/shard_map/merge/pallas_call | solution.py:384
  68.9 24.4 %layer0.1 = (f32[4,128,1024]{2,1,0:T(8,128)}, bf16[4,8,16,1024]{3,2,1,0:T(8,128)(2,1)}) custom-call(bf16[4,8,16,1024]{3,2,1,0:T(8,128)(2,1)} %get-tuple-element.9.x, bf16[2,1024,3072]{2,1,0:T(8,128)(2,1)} %qkv.3, bf16[2,1024,1024]{2,1,0:T(8,128)(2,1)} %out_w.3, f32[4,128,1024]{2,1,0:T(8,128)} %get-tuple-element.10.stream, ...), custom_call_target="tpu_custom_call" | custom-call | tf_op jit(solution)/shard_map/layer0/pallas_call | solution.py:401
  93.3 21.9 %layer1.1 = bf16[512,1024]{1,0:T(8,128)(2,1)} custom-call(bf16[4,8,16,1024]{3,2,1,0:T(8,128)(2,1)} %get-tuple-element.11.x, bf16[2,1024,3072]{2,1,0:T(8,128)(2,1)} %qkv.3, bf16[2,1024,1024]{2,1,0:T(8,128)(2,1)} %out_w.3, f32[4,128,1024]{2,1,0:T(8,128)} %get-tuple-element.12.stream, f32[4,2,64,256]{3,2,1,0:T(8,128)} %and_select_fusion.bias, ...), custom_call_target="tpu_custom_call" | custom-call | tf_op jit(solution)/shard_map/layer1/pallas_call | solution.py:401
  115.2 2.3 %copy.14 = bf16[32,16,1024]{2,1,0:T(8,128)(2,1)} copy(bf16[32,16,1024]{2,1,0:T(8,128)(2,1)} %bitcast.10) | data formatting | bytes 2097152
  (6 shorter events, 0.1 us)
Async XLA Ops:
  0.0 11.6 %copy-start = (f32[16,4,128]{2,1,0:T(4,128)S(1)}, f32[16,4,128]{2,1,0:T(4,128)}, u32[]{:S(2)}) copy-start(f32[16,4,128]{2,1,0:T(4,128)} %param.13) | copy-start | bytes 98308
  4.1 5.9 %copy-start.2 = (bf16[512,1024]{1,0:T(8,128)(2,1)S(1)}, bf16[512,1024]{1,0:T(8,128)(2,1)}, u32[]{:S(2)}) copy-start(bf16[512,1024]{1,0:T(8,128)(2,1)} %param.14) | copy-start | bytes 3145732
  4.2 54.4 %all-to-all-start = ((bf16[32,272,128]{2,1,0:T(8,128)(2,1)}), bf16[32,272,128]{2,1,0:T(8,128)(2,1)S(1)}, u32[]{:S(2)}, u32[]{:S(2)}) async-start(bf16[32,272,128]{2,1,0:T(8,128)(2,1)} %place.1), calls=%async_computation | async-start | bytes 4456448 | tf_op jit(solution)/shard_map/all_to_all | solution.py:363
  10.1 2.6 %copy-start.3 = (f32[2,1024]{1,0:T(2,128)S(1)}, f32[2,1024]{1,0:T(2,128)}, u32[]{:S(2)}) copy-start(f32[2,1024]{1,0:T(2,128)} %param.15) | copy-start | bytes 24580
  58.5 1.4 %copy-start.1 = (bf16[32,272,128]{2,1,0:T(8,128)(2,1)}, bf16[32,272,128]{2,1,0:T(8,128)(2,1)S(1)}, u32[]{:S(2)}) copy-start(bf16[32,272,128]{2,1,0:T(8,128)(2,1)S(1)} %all-to-all-done.got) | copy-start | bytes 6684676
